TPU v7x, 32 devices: a whole 2x2x4 slice. The times are simulated.
32 devices in a mesh: rows: 8 (over z, y), cols: 4 (over x, core).
Axes of the slice: x: 2, y: 2, z: 4, core: 2. Of those that a mesh axis runs over, the one named last changes fastest.
Arguments:
- points: float32 [8192, 1024], P('rows', 'cols'), may hold values from -6 to 6
- pivots: int32 [2, 512], replicated, may hold values from 0 to 8191, as said below
- targets: float32 [8192, 256], P('rows', 'cols'), may hold values from -6 to 6
Outputs:
- factor: float32 [8192, 1024], P(('rows', 'cols'))
- projection: float32 [1024, 256], P(None, 'cols')
Inputs may be any that keep to these rules, and one draw needn't show every extreme that they name: All 1024 indices of both blocks are distinct. The points of one index of rows (an aligned run of 1024 indices) hold at most 512 pivots of the two blocks together, and in every draw some index of rows holds exactly 512.
All inputs are finite; a program needn't handle non-finite values.
Results may differ from a plain program's by a relative error of at most 0.0003.
Values sent between devices are 32-bit elements; how exact they have to be, the bound alone decides.
No kernel may reach another device: no remote copies, remote signals or barrier semaphores. Data moves between devices by JAX's collectives and lax.ppermute only.
A program may use at most 64 MiB of HBM per device.

v0:
```python
import functools
import math

import jax
import jax.numpy as jnp
from jax import lax
from jax.experimental import pallas as pl
from jax.experimental.pallas import tpu as pltpu
from jax.sharding import PartitionSpec as P


HI = lax.Precision.HIGHEST
NEAR = lax.Precision.HIGH
T = 8
RIDGE = 0.001


def split(x):
    h = x.astype(jnp.bfloat16)
    r = x - h.astype(jnp.float32)
    m = r.astype(jnp.bfloat16)
    return h, m, (r - m.astype(jnp.float32)).astype(jnp.bfloat16)


def left_stack(x):
    h, m, l = split(x)
    return jnp.concatenate([h, h, m, h, m, l], axis=1)


def right_stack(x, axis):
    h, m, l = split(x)
    return jnp.concatenate([h, m, h, l, m, h], axis=axis)


def stack_dot(a, b, axis):
    return lax.dot_general(
        left_stack(a), right_stack(b, axis), (((1,), (axis,)), ((), ())), preferred_element_type=jnp.float32
    )


def diag_inverse(rows, width, sub):
    tiles = width // T
    per = sub // T
    lane = lax.broadcasted_iota(jnp.int32, (T, width), 1)
    sl = lax.broadcasted_iota(jnp.int32, (T, width), 0)
    rows = list(rows)
    scale = [None] * tiles
    for s0 in range(0, tiles, per):
        hi = s0 + per
        recs = []
        for t in range(s0, hi):
            c = {}
            for s in range(t, hi):
                for k in range(T):
                    c[s, k] = jnp.broadcast_to(rows[s][:, T * t + k : T * t + k + 1], (T, width)) + 0.0
            dv = jnp.ones((T, width), jnp.float32)
            for k in range(0, T, 2):
                col = T * t + k

                def row_of(v, i):
                    return jnp.broadcast_to(v[i : i + 1, :], (T, width))

                a = row_of(c[t, k], k)
                b = row_of(c[t, k], k + 1)
                e = row_of(c[t, k + 1], k + 1)
                det = a * e - b * b
                ra = 1.0 / a
                rd = 1.0 / det
                rad = ra * rd
                dv = jnp.where(sl == k, a, jnp.where(sl == k + 1, det * ra, dv))
                r0 = row_of(rows[t], k)
                r1 = row_of(rows[t], k + 1)
                p0 = jnp.where(lane == col, 1.0, r0)
                p1 = jnp.where(lane == col, 0.0, jnp.where(lane == col + 1, 1.0, r1))
                pv = a * p1 - b * jnp.where(lane == col + 1, 0.0, p0)
                new1 = jnp.where(lane == col + 1, 1.0, pv * ra)
                heads = {q: row_of(c[t, q], k) for q in range(k + 2, T)}
                q0 = jnp.where(lane == col + 1, 0.0, p0) * ra
                q1 = pv * rad
                tails, scaled_heads, scaled_tails = {}, {}, {}
                for s in range(t, hi):
                    c0, c1 = c[s, k], c[s, k + 1]
                    if s == t:
                        c0 = jnp.where(sl > k + 1, c0, 0.0)
                        c1 = jnp.where(sl > k + 1, c1, 0.0)
                    w = a * c1 - b * c0
                    for q in range(k + 2, T):
                        if s == t:
                            tails[q] = row_of(w, q)
                            scaled_heads[q] = heads[q] * ra
                            scaled_tails[q] = tails[q] * rad
                            c[s, q] = c[s, q] - c0 * scaled_heads[q] - (w * tails[q]) * rad
                        else:
                            c[s, q] = c[s, q] - c0 * scaled_heads[q] - w * scaled_tails[q]
                    base = rows[s]
                    if s == t:
                        base = jnp.where(((lane == col) | (lane == col + 1)) & (sl > k + 1), 0.0, base)
                        base = jnp.where(sl == k, p0, jnp.where(sl == k + 1, new1, base))
                    else:
                        base = jnp.where((lane == col) | (lane == col + 1), 0.0, base)
                    rows[s] = base - c0 * q0 - w * q1
            scale[t] = lax.rsqrt(dv)
            recs.append(1.0 / dv)
        if hi < tiles:
            x = jnp.concatenate(
                [jnp.where((lane > sl + T * t) & (lane < T * hi), 0.0, rows[t]) for t in range(s0, hi)], axis=0
            )
            w = x * jnp.concatenate(recs, axis=0)
            upd = stack_dot(w[:, T * hi :].T, x, 0)
            for s in range(hi, tiles):
                keep = jnp.where((lane >= T * s0) & (lane < T * hi), 0.0, rows[s])
                rows[s] = keep - upd[T * (s - hi) : T * (s - hi + 1), :]
    out = []
    for t in range(tiles):
        out.append(jnp.where(lane <= sl + T * t, rows[t] * scale[t], 0.0))
    return jnp.concatenate(out, axis=0)


def chol_kernel(width, sub, first, last, a_ref, o_ref, d_ref):
    n = a_ref.shape[0]
    if first == 0:
        o_ref[...] = a_ref[...]
    row = lax.broadcasted_iota(jnp.int32, (n, width), 0)

    def step(j, _):
        off = pl.multiple_of(j * width, width)
        eye = (
            lax.broadcasted_iota(jnp.int32, (width, width), 0) == lax.broadcasted_iota(jnp.int32, (width, width), 1)
        ).astype(jnp.float32)
        d_ref[...] = o_ref[pl.ds(off, width), pl.ds(off, width)] + RIDGE * eye
        m = diag_inverse([d_ref[pl.ds(T * t, T), :] for t in range(width // T)], width, sub)
        col = o_ref[:, pl.ds(off, width)]
        low = jnp.where(row >= off + width, stack_dot(col, m, 1), 0.0)
        o_ref[pl.ds(off, width), pl.ds(off, width)] = eye
        x = stack_dot(m, o_ref[pl.ds(off, width), :], 0)
        o_ref[:, pl.ds(off, width)] = jnp.where(row >= off + width, 0.0, o_ref[:, pl.ds(off, width)])
        o_ref[...] = o_ref[...] - stack_dot(low, x, 0)
        o_ref[pl.ds(off, width), :] = x
        return 0

    lax.fori_loop(first, last, step, 0)
    if last * width == n:
        rr = lax.broadcasted_iota(jnp.int32, (n, n), 0)
        cc = lax.broadcasted_iota(jnp.int32, (n, n), 1)
        o_ref[...] = jnp.where(cc <= rr, o_ref[...], 0.0)


def chol_inverse(a, first=0, last=None, width=128, sub=64):
    n = a.shape[0]
    last = n // width if last is None else last
    return pl.pallas_call(
        functools.partial(chol_kernel, width, sub, first, last),
        out_shape=jax.ShapeDtypeStruct((n, n), jnp.float32),
        in_specs=[pl.BlockSpec(memory_space=pltpu.VMEM)],
        out_specs=pl.BlockSpec(memory_space=pltpu.VMEM),
        scratch_shapes=[pltpu.VMEM((width, width), jnp.float32)],
        input_output_aliases={} if first == 0 else {0: 0},
        cost_estimate=pl.CostEstimate(flops=n * n * n * 24 * (last - first), bytes_accessed=8 * n * n, transcendentals=0),
        compiler_params=pltpu.CompilerParams(vmem_limit_bytes=32 << 20),
        name="chol",
    )(a)


def place_kernel(idx_ref, me_ref, pts_ref, out_ref):
    rows, _ = pts_ref.shape
    nrows = out_ref.shape[1]
    block = idx_ref.shape[1]
    part = block // nrows
    high, mid, tail = split(pts_ref[...])
    base = me_ref[0] * rows
    for h in range(idx_ref.shape[0]):
        idx = jnp.broadcast_to(idx_ref[h : h + 1, :] - base, (8, block)).T[:, :1]
        hot = (idx == lax.broadcasted_iota(jnp.int32, (block, rows), 1)).astype(jnp.float32).astype(jnp.bfloat16)
        total = jnp.dot(hot, tail, preferred_element_type=jnp.float32)
        total += jnp.dot(hot, mid, preferred_element_type=jnp.float32)
        total += jnp.dot(hot, high, preferred_element_type=jnp.float32)
        for r in range(nrows):
            out_ref[h, me_ref[0] ^ r] = total[r * part : (r + 1) * part, :]


def place(pivots, points):
    nrows = lax.axis_size("rows")
    blocks, block = pivots.shape
    rows, width = points.shape
    vmem = pl.BlockSpec(memory_space=pltpu.VMEM)
    return pl.pallas_call(
        place_kernel,
        out_shape=jax.ShapeDtypeStruct((blocks, nrows, block // nrows, width), jnp.float32),
        in_specs=[vmem, pl.BlockSpec(memory_space=pltpu.SMEM), vmem],
        out_specs=vmem,
        cost_estimate=pl.CostEstimate(flops=12 * block * rows * width, bytes_accessed=8 * rows * width, transcendentals=0),
        compiler_params=pltpu.CompilerParams(vmem_limit_bytes=32 << 20),
        name="place",
    )(pivots, lax.axis_index("rows").reshape(1), points)


def swap(x, mask, axis="cols"):
    size = lax.axis_size(axis)
    return lax.ppermute(x, axis, [(i, i ^ mask) for i in range(size)])


def reorder(x):
    n = x.shape[0]
    me = lax.axis_index("rows") % n
    bit = n // 2
    rest = x.shape[1:]
    while bit:
        y = x.reshape((n // (2 * bit), 2, bit) + rest)
        x = jnp.where((me & bit) != 0, y[:, ::-1], y).reshape((n,) + rest)
        bit //= 2
    return x


def scatter_places(x, after=None):
    n = x.shape[0]
    if n > 8:
        return jnp.sum(lax.all_to_all(reorder(x), "rows", 0, 0), axis=0)
    half = x.reshape((n // 2, 2) + x.shape[1:])
    s = half[:, 0] + swap(half[:, 1], 1, "rows")
    moved = [swap(s[k], 2 * k, "rows") for k in range(1, n // 2)]
    if after is not None:
        moved[0] = tie(moved[0], after)[0]
    return sum(moved, s[0])


def gather_places(x, after=None):
    n = lax.axis_size("rows")
    if n > 8:
        return gather_rows(x)
    out = jnp.stack([x] + [swap(x, 2 * k, "rows") for k in range(1, n // 2)])
    out = jnp.stack([out, swap(out, 1, "rows")], axis=1)
    out = out.reshape((n,) + x.shape)
    if after is not None:
        out = tie(out, after)[0]
    return reorder(out).reshape((n * x.shape[0],) + x.shape[1:])


def scatter_sum(x):
    return jnp.sum(lax.all_to_all(x, "rows", 0, 0), axis=0)


def gather_rows(x):
    n = lax.axis_size("rows")
    y = lax.all_to_all(jnp.broadcast_to(x[None], (n,) + x.shape), "rows", 0, 0)
    return y.reshape((n * x.shape[0],) + x.shape[1:])


def tie(*xs):
    return lax.optimization_barrier(xs)


def gauss(left, right):
    cross = lax.dot_general(left, right, (((1,), (1,)), ((), ())), precision=NEAR, preferred_element_type=jnp.float32)
    ln = jnp.sum(left * left, axis=1)
    rn = jnp.sum(right * right, axis=1)
    dist = ln[:, None] + rn[None, :] - 2.0 * cross
    return jnp.exp(-dist / (2.0 * left.shape[1]))


def mul_t(a, b):
    return lax.dot_general(a, b, (((1,), (1,)), ((), ())), precision=HI, preferred_element_type=jnp.float32)


def work(points, pivots, targets):
    rows_dev = points.shape[0]
    nrows = lax.axis_size("rows")
    ncols = lax.axis_size("cols")
    assert ncols == 4
    block = pivots.shape[1]
    kept = rows_dev // ncols
    col = lax.axis_index("cols")

    goals = targets.T

    def bundle(k):
        at = (col ^ k) * kept
        return [lax.dynamic_slice_in_dim(points, at, kept, 0), lax.dynamic_slice_in_dim(goals, at, kept, 1)]

    placed = place(pivots, points)
    far = swap(jnp.concatenate(bundle(2) + bundle(3), axis=0), 2)
    part_a = scatter_places(placed[0])
    tall = kept + goals.shape[0]
    rows_a = gather_places(part_a)
    part_b = scatter_places(placed[1], part_a)
    near = swap(jnp.concatenate(bundle(1) + [far[tall:]], axis=0), 1)
    mine = bundle(0)
    own = jnp.concatenate([mine[0], near[:kept], far[:kept], near[tall : tall + kept]], axis=1)
    goal = [mine[1], near[kept:tall], far[kept:tall], near[tall + kept :]]

    two_a = swap(rows_a, 2)
    one_a = swap(rows_a, 1)
    piv_a = jnp.concatenate([rows_a, one_a, two_a, swap(two_a, 1)], axis=1)
    kern_aa = gauss(piv_a, piv_a)
    rows_b = gather_places(part_b, kern_aa)
    kern_aa, rows_b = tie(kern_aa, rows_b)
    two_b = swap(rows_b, 2)
    one_b = swap(rows_b, 1)
    state = chol_inverse(kern_aa, 0, 3)
    state, two_b, one_b = tie(state, two_b, one_b)
    piv_b = jnp.concatenate([rows_b, one_b, two_b, swap(two_b, 1)], axis=1)
    pivs = jnp.concatenate([piv_a, piv_b], axis=0)
    kern = gauss(own, pivs)
    pieces = lax.dot_general(
        jnp.concatenate(goal, axis=0), kern, (((1,), (0,)), ((), ())), precision=HI, preferred_element_type=jnp.float32
    ).reshape(ncols, goals.shape[0], kern.shape[1])
    back = swap(jnp.concatenate([pieces[1], pieces[3]], axis=0), 1)
    deep = goals.shape[0]
    home = pieces[0] + back[:deep]
    away = pieces[2] + back[deep:]
    side = gauss(tie(piv_b, away)[0], pivs)
    state, away = tie(state, away)
    returned = swap(away, 2)
    inv_one = chol_inverse(state, 3, 4)
    inv_one, returned = tie(inv_one, returned)
    summed = home + returned
    summed = scatter_sum(summed.reshape(nrows, deep // nrows, summed.shape[1]))
    crossed = mul_t(side[:, :block], inv_one)
    schur = side[:, block:] - mul_t(crossed, crossed)
    schur, summed = tie(schur, summed)
    total = gather_rows(summed)
    inv_two = chol_inverse(schur)
    own_one = mul_t(kern[:, :block], inv_one)
    own_left = kern[:, block:] - mul_t(own_one, crossed)
    inv_two, own_one, own_left, total = tie(inv_two, own_one, own_left, total)
    tot_one = mul_t(total[:, :block], inv_one)
    tot_left = total[:, block:] - mul_t(tot_one, crossed)
    factor = jnp.concatenate([own_one, mul_t(own_left, inv_two)], axis=1)
    final = jnp.concatenate([tot_one, mul_t(tot_left, inv_two)], axis=1)
    projection = final.T * (1.0 / math.sqrt(rows_dev * nrows))
    return (factor, projection)


def solution(mesh):
    return jax.shard_map(
        work,
        mesh=mesh,
        in_specs=(P("rows", "cols"), P(), P("rows", "cols")),
        out_specs=(P(("rows", "cols"), None), P(None, "cols")),
        check_vma=False,
    )
```

profile of v0, /device:TPU:0, one launch (start us, length us, event | category | flops | bytes accessed | tf_op | source)
XLA Modules:
  0.0 137.8 jit_solution(4650743063298696281)
XLA Ops:
  0.6 1.2 copy-done
  1.9 0.7 copy-done.2
  2.6 2.1 %place.1 = f32[2,8,64,256]{3,2,1,0:T(8,128)S(1)} custom-call(s32[2,512]{1,0:T(2,128)S(1)} %copy-done.2, s32[1]{0:T(128)} %bitcast.me_ref, f32[1024,256]{1,0:T(8,128)S(1)} %copy-done), custom_call_target="tpu_custom_call" | custom-call | flops 1610612736 | bytes 2097152 | tf_op jit(solution)/shard_map/place/pallas_call | solution.py:186
  4.8 3.1 %collective-permute-start = (f32[4,64,256]{2,1,0:T(8,128)S(1)}, f32[4,64,256]{2,1,0:T(8,128)}, u32[]{:S(2)}, u32[]{:S(2)}) collective-permute-start(f32[4,64,256]{2,1,0:T(8,128)S(1)} %slice_bitcast_fusion.2), channel_id=1, source_target_pairs={{0,4},{4,0},{8,12},{12,8},{16,20},{20,16},{24,28},{28,24},{1,5},{5... | collective-permute-start | bytes 786440 | tf_op jit(solution)/shard_map/ppermute | solution.py:199
  7.9 0.7 slice_bitcast_fusion
  8.8 6.4 %collective-permute-done = f32[4,64,256]{2,1,0:T(8,128)} collective-permute-done((f32[4,64,256]{2,1,0:T(8,128)S(1)}, f32[4,64,256]{2,1,0:T(8,128)}, u32[]{:S(2)}, u32[]{:S(2)}) %collective-permute-start) | collective-permute-done | bytes 262176 | tf_op jit(solution)/shard_map/ppermute | solution.py:199
  15.2 1.0 fusion.7
  16.2 2.1 %collective-permute-start.1 = (f32[64,256]{1,0:T(8,128)S(1)}, f32[64,256]{1,0:T(8,128)S(1)}, u32[]{:S(2)}, u32[]{:S(2)}) collective-permute-start(f32[64,256]{1,0:T(8,128)S(1)} %get-tuple-element.61), channel_id=1, source_target_pairs={{0,8},{4,12},{8,0},{12,4},{16,24},{20,28},{24,16},{28,20},{1,9},{5... | collective-permute-start | bytes 196616 | tf_op jit(solution)/shard_map/ppermute | solution.py:199
  18.3 2.5 %collective-permute-start.3 = (f32[64,256]{1,0:T(8,128)S(1)}, f32[64,256]{1,0:T(8,128)S(1)}, u32[]{:S(2)}, u32[]{:S(2)}) collective-permute-start(f32[64,256]{1,0:T(8,128)S(1)} %get-tuple-element.62), channel_id=1, source_target_pairs={{0,24},{4,28},{8,16},{12,20},{16,8},{20,12},{24,0},{28,4},{1,25},{... | collective-permute-start | bytes 196616 | tf_op jit(solution)/shard_map/ppermute | solution.py:199
  20.9 0.9 pad_maximum_fusion.5
  21.8 1.5 %collective-permute-start.22 = (f32[640,256]{1,0:T(8,128)}, f32[640,256]{1,0:T(8,128)S(1)}, u32[]{:S(2)}, u32[]{:S(2)}) collective-permute-start(f32[640,256]{1,0:T(8,128)} %pad_maximum_fusion.5), channel_id=1, source_target_pairs={{0,2},{1,3},{2,0},{3,1},{4,6},{5,7},{6,4},{7,5},{8,10},{9,11},{10,... | collective-permute-start | bytes 1966088 | tf_op jit(solution)/shard_map/ppermute | solution.py:199
  23.3 1.1 collective-permute-done.3
  24.4 2.7 %collective-permute-done.2 = f32[64,256]{1,0:T(8,128)S(1)} collective-permute-done((f32[64,256]{1,0:T(8,128)S(1)}, f32[64,256]{1,0:T(8,128)S(1)}, u32[]{:S(2)}, u32[]{:S(2)}) %collective-permute-start.2) | collective-permute-done | bytes 65568 | tf_op jit(solution)/shard_map/ppermute | solution.py:199
  27.1 1.9 %collective-permute-start.6 = (f32[64,256]{1,0:T(8,128)S(1)}, f32[64,256]{1,0:T(8,128)S(1)}, u32[]{:S(2)}, u32[]{:S(2)}) collective-permute-start(f32[64,256]{1,0:T(8,128)S(1)} %fusion.24), channel_id=1, source_target_pairs={{0,24},{4,28},{8,16},{12,20},{16,8},{20,12},{24,0},{28,4},{1,25},{... | collective-permute-start | bytes 196616 | tf_op jit(solution)/shard_map/ppermute | solution.py:199
  29.0 2.6 %collective-permute-start.4 = (f32[64,256]{1,0:T(8,128)S(1)}, f32[64,256]{1,0:T(8,128)S(1)}, u32[]{:S(2)}, u32[]{:S(2)}) collective-permute-start(f32[64,256]{1,0:T(8,128)S(1)} %fusion.24), channel_id=1, source_target_pairs={{0,8},{4,12},{8,0},{12,4},{16,24},{20,28},{24,16},{28,20},{1,9},{5... | collective-permute-start | bytes 196616 | tf_op jit(solution)/shard_map/ppermute | solution.py:199
  31.6 1.0 fusion.6
  32.6 0.7 collective-permute-done.6
  33.2 1.4 %collective-permute-done.5 = f32[64,256]{1,0:T(8,128)S(1)} collective-permute-done((f32[64,256]{1,0:T(8,128)S(1)}, f32[64,256]{1,0:T(8,128)S(1)}, u32[]{:S(2)}, u32[]{:S(2)}) %collective-permute-start.5) | collective-permute-done | bytes 65568 | tf_op jit(solution)/shard_map/ppermute | solution.py:199
  34.6 0.2 collective-permute-done.4
  34.9 2.3 %collective-permute-start.7 = (f32[4,64,256]{2,1,0:T(8,128)S(1)}, f32[4,64,256]{2,1,0:T(8,128)S(1)}, u32[]{:S(2)}, u32[]{:S(2)}) collective-permute-start(f32[4,64,256]{2,1,0:T(8,128)S(1)} %get-tuple-element.60), channel_id=1, source_target_pairs={{0,4},{4,0},{8,12},{12,8},{16,20},{20,16},{24,28},{28,24},{1,5},{5... | collective-permute-start | bytes 786440 | tf_op jit(solution)/shard_map/ppermute | solution.py:199
  37.2 1.0 collective-permute-start.12
  38.2 1.6 %collective-permute-start.14 = (f32[64,256]{1,0:T(8,128)S(1)}, f32[64,256]{1,0:T(8,128)S(1)}, u32[]{:S(2)}, u32[]{:S(2)}) collective-permute-start(f32[64,256]{1,0:T(8,128)S(1)} %get-tuple-element.57), channel_id=1, source_target_pairs={{0,24},{4,28},{8,16},{12,20},{16,8},{20,12},{24,0},{28,4},{1,25},{... | collective-permute-start | bytes 196616 | tf_op jit(solution)/shard_map/ppermute | solution.py:199
  39.8 0.9 collective-permute-start.13
  40.8 0.8 collective-permute-done.12
  41.9 1.6 %collective-permute-start.9 = (f32[512,256]{1,0:T(8,128)S(1)}, f32[512,256]{1,0:T(8,128)S(1)}, u32[]{:S(2)}, u32[]{:S(2)}) collective-permute-start(f32[512,256]{1,0:T(8,128)S(1)} %bitcast.106), channel_id=1, source_target_pairs={{0,2},{1,3},{2,0},{3,1},{4,6},{5,7},{6,4},{7,5},{8,10},{9,11},{10,... | collective-permute-start | bytes 1572872 | tf_op jit(solution)/shard_map/ppermute | solution.py:199
  43.5 0.9 collective-permute-done.14
  44.3 1.4 %collective-permute-done.13 = f32[64,256]{1,0:T(8,128)S(1)} collective-permute-done((f32[64,256]{1,0:T(8,128)S(1)}, f32[64,256]{1,0:T(8,128)S(1)}, u32[]{:S(2)}, u32[]{:S(2)}) %collective-permute-start.13) | collective-permute-done | bytes 65568 | tf_op jit(solution)/shard_map/ppermute | solution.py:199
  45.7 1.9 %collective-permute-start.17 = (f32[64,256]{1,0:T(8,128)S(1)}, f32[64,256]{1,0:T(8,128)S(1)}, u32[]{:S(2)}, u32[]{:S(2)}) collective-permute-start(f32[64,256]{1,0:T(8,128)S(1)} %fusion.21), channel_id=1, source_target_pairs={{0,24},{4,28},{8,16},{12,20},{16,8},{20,12},{24,0},{28,4},{1,25},{... | collective-permute-start | bytes 196616 | tf_op jit(solution)/shard_map/ppermute | solution.py:199
  47.7 2.5 %collective-permute-start.15 = (f32[64,256]{1,0:T(8,128)S(1)}, f32[64,256]{1,0:T(8,128)S(1)}, u32[]{:S(2)}, u32[]{:S(2)}) collective-permute-start(f32[64,256]{1,0:T(8,128)S(1)} %fusion.21), channel_id=1, source_target_pairs={{0,8},{4,12},{8,0},{12,4},{16,24},{20,28},{24,16},{28,20},{1,9},{5... | collective-permute-start | bytes 196616 | tf_op jit(solution)/shard_map/ppermute | solution.py:199
  50.2 1.9 %collective-permute-done.17 = f32[64,256]{1,0:T(8,128)S(1)} collective-permute-done((f32[64,256]{1,0:T(8,128)S(1)}, f32[64,256]{1,0:T(8,128)S(1)}, u32[]{:S(2)}, u32[]{:S(2)}) %collective-permute-start.17) | collective-permute-done | bytes 65568 | tf_op jit(solution)/shard_map/ppermute | solution.py:199
  52.1 1.4 collective-permute-done.16
  53.7 2.6 %collective-permute-done.9 = f32[512,256]{1,0:T(8,128)S(1)} collective-permute-done((f32[512,256]{1,0:T(8,128)S(1)}, f32[512,256]{1,0:T(8,128)S(1)}, u32[]{:S(2)}, u32[]{:S(2)}) %collective-permute-start.9) | collective-permute-done | bytes 524320 | tf_op jit(solution)/shard_map/ppermute | solution.py:199
  56.3 3.6 %collective-permute-done.18 = f32[4,64,256]{2,1,0:T(8,128)S(1)} collective-permute-done((f32[4,64,256]{2,1,0:T(8,128)S(1)}, f32[4,64,256]{2,1,0:T(8,128)S(1)}, u32[]{:S(2)}, u32[]{:S(2)}) %collective-permute-start.18) | collective-permute-done | bytes 262176 | tf_op jit(solution)/shard_map/ppermute | solution.py:199
  60.2 0.2 multiply_reduce_fusion.2
  60.4 2.0 %multiply_exponential_fusion.2.a_ref = f32[512,512]{1,0:T(8,128)S(1)} fusion(f32[512,256]{1,0:T(8,128)S(1)} %collective-permute-done.10, f32[512,256]{1,0:T(8,128)S(1)} %collective-permute-done.9, f32[512,256]{1,0:T(8,128)S(1)} %collective-permute-done.8, f32[512,256]{1,0:T(8,128)S(1)} %bitcast.109, f32[512]{0:T(512)S(1)} %multiply_reduce_fusion.2), kind=kOutput, calls=%fused_computation.17 | convolution fusion | flops 1613496320 | bytes 3147776 | tf_op jit(solution)/shard_map/dot_general | solution.py:253
  62.7 1.4 collective-permute-start.19
  64.0 11.1 %chol.3.a_ref = f32[512,512]{1,0:T(8,128)S(1)} custom-call(f32[512,512]{1,0:T(8,128)S(1)} %multiply_exponential_fusion.2.a_ref), custom_call_target="tpu_custom_call" | custom-call | flops 9663676416 | bytes 2097152 | tf_op jit(solution)/shard_map/chol/pallas_call | solution.py:151
  75.2 1.8 %collective-permute-done.19 = f32[512,256]{1,0:T(8,128)S(1)} collective-permute-done((f32[512,256]{1,0:T(8,128)S(1)}, f32[512,256]{1,0:T(8,128)S(1)}, u32[]{:S(2)}, u32[]{:S(2)}) %collective-permute-start.19) | collective-permute-done | bytes 524320 | tf_op jit(solution)/shard_map/ppermute | solution.py:199
  77.2 1.7 %collective-permute-done.21 = f32[512,256]{1,0:T(8,128)S(1)} collective-permute-done((f32[512,256]{1,0:T(8,128)S(1)}, f32[512,256]{1,0:T(8,128)S(1)}, u32[]{:S(2)}, u32[]{:S(2)}) %collective-permute-start.21) | collective-permute-done | bytes 524320 | tf_op jit(solution)/shard_map/ppermute | solution.py:199
  79.0 2.3 %multiply_reduce_fusion = f32[1024]{0:T(1024)S(1)} fusion(f32[512,1024]{1,0:T(8,128)S(1)} %constant_dynamic-update-slice_fusion, f32[512,256]{1,0:T(8,128)S(1)} %collective-permute-done.10, f32[512,256]{1,0:T(8,128)S(1)} %collective-permute-done.9, f32[512,256]{1,0:T(8,128)S(1)} %collective-permute-done.8, f32[512,256]{1,0:T(8,128)S(1)} %bitcast.110), kind=kLoop, calls=%fused_computation.1 | loop fusion | flops 6290432 | bytes 4198400 | tf_op jit(solution)/shard_map/reduce_sum | solution.py:255
  81.3 2.2 %multiply_exponential_fusion.1 = f32[256,1024]{1,0:T(8,128)S(1)} fusion(f32[256,256]{1,0:T(8,128)S(1)} %get-tuple-element.49, f32[256,256]{1,0:T(8,128)S(1)} %slice.155, f32[256,256]{1,0:T(8,128)S(1)} %get-tuple-element.48, f32[256,256]{1,0:T(8,128)S(1)} %get-tuple-element.40, f32[1024]{0:T(1024)S(1)} %multiply_reduce_fusion, ...), kind=kOutput, calls=%fused_computation.15 | convolution fusion | flops 1616904192 | bytes 6296576 | tf_op jit(solution)/shard_map/dot_general | solution.py:253
  83.5 1.0 fusion.8
  84.9 1.8 %collective-permute-done.24 = f32[128,1024]{1,0:T(8,128)S(1)} collective-permute-done((f32[128,1024]{1,0:T(8,128)S(1)}, f32[128,1024]{1,0:T(8,128)S(1)}, u32[]{:S(2)}, u32[]{:S(2)}) %collective-permute-start.24) | collective-permute-done | bytes 524320 | tf_op jit(solution)/shard_map/ppermute | solution.py:199
  86.7 0.2 multiply_reduce_fusion.1
  86.9 1.4 collective-permute-start.25
  88.2 5.1 %multiply_exponential_fusion = f32[512,1024]{1,0:T(8,128)} fusion(f32[512,1024]{1,0:T(8,128)S(1)} %constant_dynamic-update-slice_fusion, f32[1024]{0:T(1024)S(1)} %multiply_reduce_fusion, f32[512]{0:T(512)S(1)} %multiply_reduce_fusion.1, f32[512,256]{1,0:T(8,128)S(1)} %collective-permute-done.10, f32[512,256]{1,0:T(8,128)S(1)} %collective-permute-done.9, ...), kind=kOutput, calls=%fused_computation.3 | convolution fusion | flops 3228041216 | bytes 6297600 | tf_op jit(solution)/shard_map/dot_general | solution.py:253
  93.3 3.6 %chol.4 = f32[512,512]{1,0:T(8,128)S(1)} custom-call(f32[512,512]{1,0:T(8,128)S(1)} %chol.3.a_ref), custom_call_target="tpu_custom_call", output_to_operand_aliasing={{}: (0, {})} | custom-call | flops 3221225472 | bytes 2097152 | tf_op jit(solution)/shard_map/chol/pallas_call | solution.py:151
  97.0 0.8 fusion.5
  97.7 3.7 %all-to-all-start = ((f32[8,8,1024]{2,1,0:T(8,128)}), f32[8,8,1024]{2,1,0:T(8,128)S(1)}, u32[]{:S(2)}, u32[]{:S(2)}) async-start(f32[8,8,1024]{2,1,0:T(8,128)} %fusion.5), calls=%async_computation | async-start | bytes 524288 | tf_op jit(solution)/shard_map/all_to_all | solution.py:239
  101.5 1.1 fusion.2
  102.5 0.5 copy-done.6
  103.1 1.9 %fusion = f32[512,512]{1,0:T(8,128)S(1)} fusion(f32[512,512]{1,0:T(8,128)S(1)} %chol.4, f32[512,1024]{1,0:T(8,128)S(1)} %copy-done.6), kind=kOutput, calls=%fused_computation.10 | convolution fusion | flops 1610612736 | bytes 3145728 | tf_op jit(solution)/shard_map/dot_general | solution.py:261
  104.9 1.9 %convolution_subtract_fusion = f32[256,512]{1,0:T(8,128)} fusion(f32[256,512]{1,0:T(8,128)S(1)} %fusion.2, f32[512,512]{1,0:T(8,128)S(1)} %fusion, f32[256,1024]{1,0:T(8,128)S(1)} %multiply_exponential_fusion.1), kind=kOutput, calls=%fused_computation.8 | convolution fusion | flops 805437440 | bytes 2621440 | tf_op jit(solution)/shard_map/dot_general | solution.py:261
  106.8 1.9 %slice_subtract_fusion.a_ref = f32[512,512]{1,0:T(8,128)S(1)} fusion(f32[512,1024]{1,0:T(8,128)S(1)} %copy-done.6, f32[512,512]{1,0:T(8,128)S(1)} %fusion), kind=kOutput, calls=%fused_computation.12 | convolution fusion | flops 1610874880 | bytes 4194304 | tf_op jit(solution)/shard_map/dot_general | solution.py:261
  108.7 1.7 %all-to-all-done = f32[8,8,1024]{2,1,0:T(8,128)S(1)} async-done(((f32[8,8,1024]{2,1,0:T(8,128)}), f32[8,8,1024]{2,1,0:T(8,128)S(1)}, u32[]{:S(2)}, u32[]{:S(2)}) %all-to-all-start) | async-done | bytes 262176 | tf_op jit(solution)/shard_map/all_to_all | solution.py:239
  110.4 0.7 broadcast_in_dim.2
  111.2 4.3 %all-to-all-start.1 = ((f32[8,8,1024]{2,1,0:T(8,128)}), f32[8,8,1024]{2,1,0:T(8,128)S(1)}, u32[]{:S(2)}, u32[]{:S(2)}) async-start(f32[8,8,1024]{2,1,0:T(8,128)} %broadcast_in_dim.2), calls=%async_computation.1 | async-start | bytes 524288 | tf_op jit(solution)/shard_map/all_to_all | solution.py:244
  115.4 14.9 %chol.5 = f32[512,512]{1,0:T(8,128)S(1)} custom-call(f32[512,512]{1,0:T(8,128)S(1)} %slice_subtract_fusion.a_ref), custom_call_target="tpu_custom_call" | custom-call | flops 12884901888 | bytes 2097152 | tf_op jit(solution)/shard_map/chol/pallas_call | solution.py:151
  130.3 1.1 fusion.17
  131.5 2.3 %convolution_subtract_fusion.1 = f32[64,512]{1,0:T(8,128)S(1)} fusion(f32[64,512]{1,0:T(8,128)S(1)} %fusion.17, f32[512,512]{1,0:T(8,128)} %copy-done.3, f32[64,1024]{1,0:T(8,128)S(1)} %bitcast.127), kind=kOutput, calls=%fused_computation.9 | convolution fusion | flops 201359360 | bytes 1441792 | tf_op jit(solution)/shard_map/dot_general | solution.py:261
  133.8 1.1 fusion.35
  134.9 0.7 fusion.16
  135.7 1.0 fusion.34
  136.7 1.1 pad_maximum_fusion.4
  (73 shorter events, 2.1 us)
Async XLA Ops:
  0.6 1.2 copy-start
  1.9 0.7 copy-start.2
  4.7 4.0 %copy-start.9 = (f32[1024,64]{0,1:T(8,128)S(1)}, f32[1024,64]{0,1:T(8,128)}, u32[]{:S(2)}) copy-start(f32[1024,64]{0,1:T(8,128)} %param.5) | copy-start | bytes 786436
  4.7 4.0 %copy-start.1 = (f32[1024,256]{1,0:T(8,128)S(1)}, f32[1024,256]{1,0:T(8,128)}, u32[]{:S(2)}) copy-start(f32[1024,256]{1,0:T(8,128)} %pts_ref.1) | copy-start | bytes 3145732
  4.8 10.3 %collective-permute-start = (f32[4,64,256]{2,1,0:T(8,128)S(1)}, f32[4,64,256]{2,1,0:T(8,128)}, u32[]{:S(2)}, u32[]{:S(2)}) collective-permute-start(f32[4,64,256]{2,1,0:T(8,128)S(1)} %slice_bitcast_fusion.2), channel_id=1, source_target_pairs={{0,4},{4,0},{8,12},{12,8},{16,20},{20,16},{24,28},{28,24},{1,5},{5... | collective-permute-start | bytes 786440 | tf_op jit(solution)/shard_map/ppermute | solution.py:199
  8.6 22.9 %collective-permute-start.11 = (f32[4,64,256]{2,1,0:T(8,128)}, f32[4,64,256]{2,1,0:T(8,128)}, u32[]{:S(2)}, u32[]{:S(2)}) collective-permute-start(f32[4,64,256]{2,1,0:T(8,128)} %slice_bitcast_fusion), channel_id=1, source_target_pairs={{0,4},{4,0},{8,12},{12,8},{16,20},{20,16},{24,28},{28,24},{1,5},{5... | collective-permute-start | bytes 786440 | tf_op jit(solution)/shard_map/ppermute | solution.py:199
  16.2 7.1 %collective-permute-start.1 = (f32[64,256]{1,0:T(8,128)S(1)}, f32[64,256]{1,0:T(8,128)S(1)}, u32[]{:S(2)}, u32[]{:S(2)}) collective-permute-start(f32[64,256]{1,0:T(8,128)S(1)} %get-tuple-element.61), channel_id=1, source_target_pairs={{0,8},{4,12},{8,0},{12,4},{16,24},{20,28},{24,16},{28,20},{1,9},{5... | collective-permute-start | bytes 196616 | tf_op jit(solution)/shard_map/ppermute | solution.py:199
  18.3 6.1 %collective-permute-start.3 = (f32[64,256]{1,0:T(8,128)S(1)}, f32[64,256]{1,0:T(8,128)S(1)}, u32[]{:S(2)}, u32[]{:S(2)}) collective-permute-start(f32[64,256]{1,0:T(8,128)S(1)} %get-tuple-element.62), channel_id=1, source_target_pairs={{0,24},{4,28},{8,16},{12,20},{16,8},{20,12},{24,0},{28,4},{1,25},{... | collective-permute-start | bytes 196616 | tf_op jit(solution)/shard_map/ppermute | solution.py:199
  20.8 6.3 %collective-permute-start.2 = (f32[64,256]{1,0:T(8,128)S(1)}, f32[64,256]{1,0:T(8,128)S(1)}, u32[]{:S(2)}, u32[]{:S(2)}) collective-permute-start(f32[64,256]{1,0:T(8,128)S(1)} %get-tuple-element.63), channel_id=1, source_target_pairs={{0,16},{4,20},{8,24},{12,28},{16,0},{20,4},{24,8},{28,12},{1,17},{... | collective-permute-start | bytes 196616 | tf_op jit(solution)/shard_map/ppermute | solution.py:199
  21.8 19.7 %collective-permute-start.22 = (f32[640,256]{1,0:T(8,128)}, f32[640,256]{1,0:T(8,128)S(1)}, u32[]{:S(2)}, u32[]{:S(2)}) collective-permute-start(f32[640,256]{1,0:T(8,128)} %pad_maximum_fusion.5), channel_id=1, source_target_pairs={{0,2},{1,3},{2,0},{3,1},{4,6},{5,7},{6,4},{7,5},{8,10},{9,11},{10,... | collective-permute-start | bytes 1966088 | tf_op jit(solution)/shard_map/ppermute | solution.py:199
  27.1 6.1 %collective-permute-start.6 = (f32[64,256]{1,0:T(8,128)S(1)}, f32[64,256]{1,0:T(8,128)S(1)}, u32[]{:S(2)}, u32[]{:S(2)}) collective-permute-start(f32[64,256]{1,0:T(8,128)S(1)} %fusion.24), channel_id=1, source_target_pairs={{0,24},{4,28},{8,16},{12,20},{16,8},{20,12},{24,0},{28,4},{1,25},{... | collective-permute-start | bytes 196616 | tf_op jit(solution)/shard_map/ppermute | solution.py:199
  29.0 5.6 %collective-permute-start.5 = (f32[64,256]{1,0:T(8,128)S(1)}, f32[64,256]{1,0:T(8,128)S(1)}, u32[]{:S(2)}, u32[]{:S(2)}) collective-permute-start(f32[64,256]{1,0:T(8,128)S(1)} %fusion.24), channel_id=1, source_target_pairs={{0,16},{4,20},{8,24},{12,28},{16,0},{20,4},{24,8},{28,12},{1,17},{... | collective-permute-start | bytes 196616 | tf_op jit(solution)/shard_map/ppermute | solution.py:199
  29.0 5.9 %collective-permute-start.4 = (f32[64,256]{1,0:T(8,128)S(1)}, f32[64,256]{1,0:T(8,128)S(1)}, u32[]{:S(2)}, u32[]{:S(2)}) collective-permute-start(f32[64,256]{1,0:T(8,128)S(1)} %fusion.24), channel_id=1, source_target_pairs={{0,8},{4,12},{8,0},{12,4},{16,24},{20,28},{24,16},{28,20},{1,9},{5... | collective-permute-start | bytes 196616 | tf_op jit(solution)/shard_map/ppermute | solution.py:199
  34.9 6.8 %collective-permute-start.7 = (f32[4,64,256]{2,1,0:T(8,128)S(1)}, f32[4,64,256]{2,1,0:T(8,128)S(1)}, u32[]{:S(2)}, u32[]{:S(2)}) collective-permute-start(f32[4,64,256]{2,1,0:T(8,128)S(1)} %get-tuple-element.60), channel_id=1, source_target_pairs={{0,4},{4,0},{8,12},{12,8},{16,20},{20,16},{24,28},{28,24},{1,5},{5... | collective-permute-start | bytes 786440 | tf_op jit(solution)/shard_map/ppermute | solution.py:199
  37.2 4.3 %collective-permute-start.12 = (f32[64,256]{1,0:T(8,128)S(1)}, f32[64,256]{1,0:T(8,128)S(1)}, u32[]{:S(2)}, u32[]{:S(2)}) collective-permute-start(f32[64,256]{1,0:T(8,128)S(1)} %get-tuple-element.56), channel_id=1, source_target_pairs={{0,8},{4,12},{8,0},{12,4},{16,24},{20,28},{24,16},{28,20},{1,9},{5... | collective-permute-start | bytes 196616 | tf_op jit(solution)/shard_map/ppermute | solution.py:199
  38.2 6.1 %collective-permute-start.14 = (f32[64,256]{1,0:T(8,128)S(1)}, f32[64,256]{1,0:T(8,128)S(1)}, u32[]{:S(2)}, u32[]{:S(2)}) collective-permute-start(f32[64,256]{1,0:T(8,128)S(1)} %get-tuple-element.57), channel_id=1, source_target_pairs={{0,24},{4,28},{8,16},{12,20},{16,8},{20,12},{24,0},{28,4},{1,25},{... | collective-permute-start | bytes 196616 | tf_op jit(solution)/shard_map/ppermute | solution.py:199
  39.8 5.9 %collective-permute-start.13 = (f32[64,256]{1,0:T(8,128)S(1)}, f32[64,256]{1,0:T(8,128)S(1)}, u32[]{:S(2)}, u32[]{:S(2)}) collective-permute-start(f32[64,256]{1,0:T(8,128)S(1)} %get-tuple-element.58), channel_id=1, source_target_pairs={{0,16},{4,20},{8,24},{12,28},{16,0},{20,4},{24,8},{28,12},{1,17},{... | collective-permute-start | bytes 196616 | tf_op jit(solution)/shard_map/ppermute | solution.py:199
  41.5 14.8 %copy-start.8 = (f32[640,256]{1,0:T(8,128)}, f32[640,256]{1,0:T(8,128)S(1)}, u32[]{:S(2)}) copy-start(f32[640,256]{1,0:T(8,128)S(1)} %collective-permute-done.22) | copy-start | bytes 1966084
  41.6 18.4 %collective-permute-start.23 = (f32[640,256]{1,0:T(8,128)S(1)}, f32[640,256]{1,0:T(8,128)S(1)}, u32[]{:S(2)}, u32[]{:S(2)}) collective-permute-start(f32[640,256]{1,0:T(8,128)S(1)} %pad_maximum_fusion.6), channel_id=1, source_target_pairs={{0,1},{1,0},{2,3},{3,2},{4,5},{5,4},{6,7},{7,6},{8,9},{9,8},{10,11... | collective-permute-start | bytes 1966088 | tf_op jit(solution)/shard_map/ppermute | solution.py:199
  41.9 14.4 %collective-permute-start.9 = (f32[512,256]{1,0:T(8,128)S(1)}, f32[512,256]{1,0:T(8,128)S(1)}, u32[]{:S(2)}, u32[]{:S(2)}) collective-permute-start(f32[512,256]{1,0:T(8,128)S(1)} %bitcast.106), channel_id=1, source_target_pairs={{0,2},{1,3},{2,0},{3,1},{4,6},{5,7},{6,4},{7,5},{8,10},{9,11},{10,... | collective-permute-start | bytes 1572872 | tf_op jit(solution)/shard_map/ppermute | solution.py:199
  45.7 6.3 %collective-permute-start.17 = (f32[64,256]{1,0:T(8,128)S(1)}, f32[64,256]{1,0:T(8,128)S(1)}, u32[]{:S(2)}, u32[]{:S(2)}) collective-permute-start(f32[64,256]{1,0:T(8,128)S(1)} %fusion.21), channel_id=1, source_target_pairs={{0,24},{4,28},{8,16},{12,20},{16,8},{20,12},{24,0},{28,4},{1,25},{... | collective-permute-start | bytes 196616 | tf_op jit(solution)/shard_map/ppermute | solution.py:199
  47.7 5.8 %collective-permute-start.16 = (f32[64,256]{1,0:T(8,128)S(1)}, f32[64,256]{1,0:T(8,128)S(1)}, u32[]{:S(2)}, u32[]{:S(2)}) collective-permute-start(f32[64,256]{1,0:T(8,128)S(1)} %fusion.21), channel_id=1, source_target_pairs={{0,16},{4,20},{8,24},{12,28},{16,0},{20,4},{24,8},{28,12},{1,17},{... | collective-permute-start | bytes 196616 | tf_op jit(solution)/shard_map/ppermute | solution.py:199
  47.7 5.8 %collective-permute-start.15 = (f32[64,256]{1,0:T(8,128)S(1)}, f32[64,256]{1,0:T(8,128)S(1)}, u32[]{:S(2)}, u32[]{:S(2)}) collective-permute-start(f32[64,256]{1,0:T(8,128)S(1)} %fusion.21), channel_id=1, source_target_pairs={{0,8},{4,12},{8,0},{12,4},{16,24},{20,28},{24,16},{28,20},{1,9},{5... | collective-permute-start | bytes 196616 | tf_op jit(solution)/shard_map/ppermute | solution.py:199
  53.5 6.4 %collective-permute-start.18 = (f32[4,64,256]{2,1,0:T(8,128)S(1)}, f32[4,64,256]{2,1,0:T(8,128)S(1)}, u32[]{:S(2)}, u32[]{:S(2)}) collective-permute-start(f32[4,64,256]{2,1,0:T(8,128)S(1)} %get-tuple-element.55), channel_id=1, source_target_pairs={{0,4},{4,0},{8,12},{12,8},{16,20},{20,16},{24,28},{28,24},{1,5},{5... | collective-permute-start | bytes 786440 | tf_op jit(solution)/shard_map/ppermute | solution.py:199
  53.6 6.6 %collective-permute-start.8 = (f32[512,256]{1,0:T(8,128)S(1)}, f32[512,256]{1,0:T(8,128)S(1)}, u32[]{:S(2)}, u32[]{:S(2)}) collective-permute-start(f32[512,256]{1,0:T(8,128)S(1)} %bitcast.107), channel_id=1, source_target_pairs={{0,1},{1,0},{2,3},{3,2},{4,5},{5,4},{6,7},{7,6},{8,9},{9,8},{10,11... | collective-permute-start | bytes 1572872 | tf_op jit(solution)/shard_map/ppermute | solution.py:199
  56.3 3.9 %collective-permute-start.10 = (f32[512,256]{1,0:T(8,128)S(1)}, f32[512,256]{1,0:T(8,128)S(1)}, u32[]{:S(2)}, u32[]{:S(2)}) collective-permute-start(f32[512,256]{1,0:T(8,128)S(1)} %collective-permute-done.9), channel_id=1, source_target_pairs={{0,1},{1,0},{2,3},{3,2},{4,5},{5,4},{6,7},{7,6},{8,9},{9,8},{10,11... | collective-permute-start | bytes 1572872 | tf_op jit(solution)/shard_map/ppermute | solution.py:199
  62.6 12.6 %collective-permute-start.20 = (f32[512,256]{1,0:T(8,128)S(1)}, f32[512,256]{1,0:T(8,128)S(1)}, u32[]{:S(2)}, u32[]{:S(2)}) collective-permute-start(f32[512,256]{1,0:T(8,128)S(1)} %bitcast.117), channel_id=1, source_target_pairs={{0,1},{1,0},{2,3},{3,2},{4,5},{5,4},{6,7},{7,6},{8,9},{9,8},{10,11... | collective-permute-start | bytes 1572872 | tf_op jit(solution)/shard_map/ppermute | solution.py:199
  62.7 14.3 %collective-permute-start.19 = (f32[512,256]{1,0:T(8,128)S(1)}, f32[512,256]{1,0:T(8,128)S(1)}, u32[]{:S(2)}, u32[]{:S(2)}) collective-permute-start(f32[512,256]{1,0:T(8,128)S(1)} %bitcast.118), channel_id=1, source_target_pairs={{0,2},{1,3},{2,0},{3,1},{4,6},{5,7},{6,4},{7,5},{8,10},{9,11},{10,... | collective-permute-start | bytes 1572872 | tf_op jit(solution)/shard_map/ppermute | solution.py:199
  77.0 1.9 %collective-permute-start.21 = (f32[512,256]{1,0:T(8,128)S(1)}, f32[512,256]{1,0:T(8,128)S(1)}, u32[]{:S(2)}, u32[]{:S(2)}) collective-permute-start(f32[512,256]{1,0:T(8,128)S(1)} %collective-permute-done.19), channel_id=1, source_target_pairs={{0,1},{1,0},{2,3},{3,2},{4,5},{5,4},{6,7},{7,6},{8,9},{9,8},{10,11... | collective-permute-start | bytes 1572872 | tf_op jit(solution)/shard_map/ppermute | solution.py:199
  81.3 2.2 %slice-start = ((f32[640,256]{1,0:T(8,128)}), f32[64,256]{1,0:T(8,128)S(1)}, s32[]{:S(2)}) async-start(f32[640,256]{1,0:T(8,128)} %copy-done.8), calls=%async_computation.2 | async-start | bytes 131072 | tf_op jit(solution)/shard_map/slice | solution.py:288
  84.7 2.0 %collective-permute-start.24 = (f32[128,1024]{1,0:T(8,128)S(1)}, f32[128,1024]{1,0:T(8,128)S(1)}, u32[]{:S(2)}, u32[]{:S(2)}) collective-permute-start(f32[128,1024]{1,0:T(8,128)S(1)} %pad_maximum_fusion.12), channel_id=1, source_target_pairs={{0,1},{1,0},{2,3},{3,2},{4,5},{5,4},{6,7},{7,6},{8,9},{9,8},{10,11... | collective-permute-start | bytes 1572872 | tf_op jit(solution)/shard_map/ppermute | solution.py:199
  86.9 10.1 %collective-permute-start.25 = (f32[64,1024]{1,0:T(8,128)S(1)}, f32[64,1024]{1,0:T(8,128)S(1)}, u32[]{:S(2)}, u32[]{:S(2)}) collective-permute-start(f32[64,1024]{1,0:T(8,128)S(1)} %slice_add_fusion.1), channel_id=1, source_target_pairs={{0,2},{1,3},{2,0},{3,1},{4,6},{5,7},{6,4},{7,5},{8,10},{9,11},{10,... | collective-permute-start | bytes 786440 | tf_op jit(solution)/shard_map/ppermute | solution.py:199
  97.7 12.7 %all-to-all-start = ((f32[8,8,1024]{2,1,0:T(8,128)}), f32[8,8,1024]{2,1,0:T(8,128)S(1)}, u32[]{:S(2)}, u32[]{:S(2)}) async-start(f32[8,8,1024]{2,1,0:T(8,128)} %fusion.5), calls=%async_computation | async-start | bytes 524288 | tf_op jit(solution)/shard_map/all_to_all | solution.py:239
  101.5 1.6 %copy-start.6 = (f32[512,1024]{1,0:T(8,128)S(1)}, f32[512,1024]{1,0:T(8,128)}, u32[]{:S(2)}) copy-start(f32[512,1024]{1,0:T(8,128)} %multiply_exponential_fusion) | copy-start | bytes 6291460
  103.1 3.7 %copy-start.4 = (f32[256,512]{1,0:T(8,128)}, f32[256,512]{1,0:T(8,128)S(1)}, u32[]{:S(2)}) copy-start(f32[256,512]{1,0:T(8,128)S(1)} %fusion.2) | copy-start | bytes 1572868
  104.9 3.7 %copy-start.3 = (f32[512,512]{1,0:T(8,128)}, f32[512,512]{1,0:T(8,128)S(1)}, u32[]{:S(2)}) copy-start(f32[512,512]{1,0:T(8,128)S(1)} %fusion) | copy-start | bytes 3145732
  111.2 19.2 %all-to-all-start.1 = ((f32[8,8,1024]{2,1,0:T(8,128)}), f32[8,8,1024]{2,1,0:T(8,128)S(1)}, u32[]{:S(2)}, u32[]{:S(2)}) async-start(f32[8,8,1024]{2,1,0:T(8,128)} %broadcast_in_dim.2), calls=%async_computation.1 | async-start | bytes 524288 | tf_op jit(solution)/shard_map/all_to_all | solution.py:244
  130.3 5.3 %copy-start.7 = (f32[256,512]{1,0:T(8,128)S(1)}, f32[256,512]{1,0:T(8,128)}, u32[]{:S(2)}) copy-start(f32[256,512]{1,0:T(8,128)} %convolution_subtract_fusion) | copy-start | bytes 1572868
  133.8 2.9 %copy-start.5 = (f32[256,512]{1,0:T(8,128)S(1)}, f32[256,512]{1,0:T(8,128)}, u32[]{:S(2)}) copy-start(f32[256,512]{1,0:T(8,128)} %copy-done.4) | copy-start | bytes 1572868
where the time goes:
time: 138 us
  starting transfers between devices  36.8 us (27%)
  waiting for transfers between devices  32.1 us (23%)
  Pallas kernels  31.8 us (23%)
  matrix products  22.6 us (16%)
  other arithmetic  8.89 us (6%)
  local copies, waits for them, and re-layouts  4.56 us (3%)
    ppermute x26, waiting for transfers between devices, swap(): return lax.ppermute(x, axis, [(i, i ^ mask) for i in range(size)])  30.3 us
    pallas_call x3, Pallas kernels, chol_inverse(): pl.pallas_call(functools.partial(chol_kernel, width, sub, first, last), o...  29.6 us
    ppermute x26, starting transfers between devices, swap(): return lax.ppermute(x, axis, [(i, i ^ mask) for i in range(size)])  28.8 us
    dot_general x8, matrix products, mul_t(): lax.dot_general(a, b, (((1,), (1,)), ((), ())), precision=HI, preferred_e...  12.3 us
    dot_general x3, matrix products, gauss(): lax.dot_general(left, right, (((1,), (1,)), ((), ())), precision=NEAR, pr...  9.3 us
    all_to_all x1, starting transfers between devices, gather_rows(): y = lax.all_to_all(jnp.broadcast_to(x[None], (n,) + x.shape), 'rows', 0, 0)  4.27 us
    all_to_all x1, starting transfers between devices, scatter_sum(): return jnp.sum(lax.all_to_all(x, 'rows', 0, 0), axis=0)  3.72 us
  transfers between devices with their start and end apart: 28, of which 17 were waited for; matrix products, arithmetic and copies ran while one was open for 12% of the time, Pallas kernels for 22%

commit v1 on v0

--- a/solution.py
+++ b/solution.py
@@ -106,7 +106,11 @@
                 [jnp.where((lane > sl + T * t) & (lane < T * hi), 0.0, rows[t]) for t in range(s0, hi)], axis=0
             )
             w = x * jnp.concatenate(recs, axis=0)
-            upd = stack_dot(w[:, T * hi :].T, x, 0)
+            h, m, l = split(w)
+            left = jnp.concatenate([h, h, m, h, m, l], axis=0)
+            upd = lax.dot_general(
+                left, right_stack(x, 0), (((0,), (0,)), ((), ())), preferred_element_type=jnp.float32
+            )[T * hi :]
             for s in range(hi, tiles):
                 keep = jnp.where((lane >= T * s0) & (lane < T * hi), 0.0, rows[s])
                 rows[s] = keep - upd[T * (s - hi) : T * (s - hi + 1), :]
@@ -116,11 +120,9 @@
     return jnp.concatenate(out, axis=0)
 
 
-def chol_kernel(width, sub, first, last, a_ref, o_ref, d_ref):
-    n = a_ref.shape[0]
-    if first == 0:
-        o_ref[...] = a_ref[...]
-    row = lax.broadcasted_iota(jnp.int32, (n, width), 0)
+def chol_steps(width, sub, first, last, o_ref, d_ref):
+    n = o_ref.shape[0]
+    row = lax.broadcasted_iota(jnp.int32, (n - width, width), 0) + width
 
     def step(j, _):
         off = pl.multiple_of(j * width, width)
@@ -129,13 +131,17 @@
         ).astype(jnp.float32)
         d_ref[...] = o_ref[pl.ds(off, width), pl.ds(off, width)] + RIDGE * eye
         m = diag_inverse([d_ref[pl.ds(T * t, T), :] for t in range(width // T)], width, sub)
-        col = o_ref[:, pl.ds(off, width)]
-        low = jnp.where(row >= off + width, stack_dot(col, m, 1), 0.0)
         o_ref[pl.ds(off, width), pl.ds(off, width)] = eye
         x = stack_dot(m, o_ref[pl.ds(off, width), :], 0)
-        o_ref[:, pl.ds(off, width)] = jnp.where(row >= off + width, 0.0, o_ref[:, pl.ds(off, width)])
-        o_ref[...] = o_ref[...] - stack_dot(low, x, 0)
         o_ref[pl.ds(off, width), :] = x
+
+        @pl.when(off + width < n)
+        def _():
+            col = o_ref[width:, pl.ds(off, width)]
+            low = jnp.where(row >= off + width, stack_dot(col, m, 1), 0.0)
+            o_ref[width:, pl.ds(off, width)] = jnp.where(row >= off + width, 0.0, col)
+            o_ref[width:, :] = o_ref[width:, :] - stack_dot(low, x, 0)
+
         return 0
 
     lax.fori_loop(first, last, step, 0)
@@ -145,20 +151,90 @@
         o_ref[...] = jnp.where(cc <= rr, o_ref[...], 0.0)
 
 
-def chol_inverse(a, first=0, last=None, width=128, sub=64):
+def chol_kernel(width, sub, first, last, a_ref, o_ref, d_ref):
+    del a_ref
+    chol_steps(width, sub, first, last, o_ref, d_ref)
+
+
+VMEM = pl.BlockSpec(memory_space=pltpu.VMEM)
+
+
+def chol_inverse(a, first, last, width=128, sub=64):
     n = a.shape[0]
-    last = n // width if last is None else last
     return pl.pallas_call(
         functools.partial(chol_kernel, width, sub, first, last),
         out_shape=jax.ShapeDtypeStruct((n, n), jnp.float32),
-        in_specs=[pl.BlockSpec(memory_space=pltpu.VMEM)],
-        out_specs=pl.BlockSpec(memory_space=pltpu.VMEM),
+        in_specs=[VMEM],
+        out_specs=VMEM,
         scratch_shapes=[pltpu.VMEM((width, width), jnp.float32)],
-        input_output_aliases={} if first == 0 else {0: 0},
+        input_output_aliases={0: 0},
         cost_estimate=pl.CostEstimate(flops=n * n * n * 24 * (last - first), bytes_accessed=8 * n * n, transcendentals=0),
-        compiler_params=pltpu.CompilerParams(vmem_limit_bytes=32 << 20),
+        compiler_params=pltpu.CompilerParams(vmem_limit_bytes=12 << 20),
         name="chol",
     )(a)
+
+
+def schur_kernel(side_ref, one_ref, cross_ref, schur_ref):
+    n = one_ref.shape[0]
+    crossed = stack_dot(side_ref[:, :n], one_ref[...], 1)
+    cross_ref[...] = crossed
+    schur_ref[...] = side_ref[:, n:] - stack_dot(crossed, crossed, 1)
+
+
+def schur_of(side, one):
+    n = one.shape[0]
+    shape = jax.ShapeDtypeStruct((n, n), jnp.float32)
+    return pl.pallas_call(
+        schur_kernel,
+        out_shape=(shape, shape),
+        in_specs=[VMEM] * 2,
+        out_specs=(VMEM, VMEM),
+        cost_estimate=pl.CostEstimate(flops=24 * n * n * n, bytes_accessed=20 * n * n, transcendentals=0),
+        compiler_params=pltpu.CompilerParams(vmem_limit_bytes=24 << 20),
+        name="schur",
+    )(side, one)
+
+
+def finish_kernel(
+    width, sub, first, scale, a_ref, k1_ref, k2_ref, tot_ref, one_ref, cross_ref, factor_ref, proj_ref, two_ref, d_ref, w_ref
+):
+    n = one_ref.shape[0]
+    rows = k1_ref.shape[0]
+    del a_ref
+    chol_steps(width, sub, first, n // width, two_ref, d_ref)
+    w_ref[:rows, :n] = k1_ref[...]
+    w_ref[:rows, n:] = k2_ref[...]
+    w_ref[rows:, :] = tot_ref[...]
+    one = stack_dot(w_ref[:, :n], one_ref[...], 1)
+    factor_ref[:, :n] = one[:rows]
+    proj_ref[:, :n] = one[rows:] * scale
+    left = w_ref[:, n:] - stack_dot(one, cross_ref[...], 1)
+    two = stack_dot(left, two_ref[...], 1)
+    factor_ref[:, n:] = two[:rows]
+    proj_ref[:, n:] = two[rows:] * scale
+
+
+def finish(scale, state, kern_a, kern_b, tot, one, crossed, first, width=128, sub=64):
+    rows = kern_a.shape[0]
+    deep, both = tot.shape
+    return pl.pallas_call(
+        functools.partial(finish_kernel, width, sub, first, scale),
+        out_shape=(
+            jax.ShapeDtypeStruct((rows, both), jnp.float32),
+            jax.ShapeDtypeStruct((deep, both), jnp.float32),
+            jax.ShapeDtypeStruct(state.shape, jnp.float32),
+        ),
+        in_specs=[VMEM] * 6,
+        out_specs=(VMEM, VMEM, VMEM),
+        input_output_aliases={0: 2},
+        scratch_shapes=[
+            pltpu.VMEM((width, width), jnp.float32),
+            pltpu.VMEM((rows + deep, both), jnp.float32),
+        ],
+        cost_estimate=pl.CostEstimate(flops=9 * (rows + deep) * both * both // 2, bytes_accessed=16 * rows * both, transcendentals=0),
+        compiler_params=pltpu.CompilerParams(vmem_limit_bytes=24 << 20),
+        name="finish",
+    )(state, kern_a, kern_b, tot, one, crossed)[:2]
 
 
 def place_kernel(idx_ref, me_ref, pts_ref, out_ref):
@@ -199,9 +275,8 @@
     return lax.ppermute(x, axis, [(i, i ^ mask) for i in range(size)])
 
 
-def reorder(x):
+def reorder(x, me):
     n = x.shape[0]
-    me = lax.axis_index("rows") % n
     bit = n // 2
     rest = x.shape[1:]
     while bit:
@@ -214,7 +289,7 @@
 def scatter_places(x, after=None):
     n = x.shape[0]
     if n > 8:
-        return jnp.sum(lax.all_to_all(reorder(x), "rows", 0, 0), axis=0)
+        return jnp.sum(lax.all_to_all(reorder(x, lax.axis_index("rows")), "rows", 0, 0), axis=0)
     half = x.reshape((n // 2, 2) + x.shape[1:])
     s = half[:, 0] + swap(half[:, 1], 1, "rows")
     moved = [swap(s[k], 2 * k, "rows") for k in range(1, n // 2)]
@@ -232,7 +307,7 @@
     out = out.reshape((n,) + x.shape)
     if after is not None:
         out = tie(out, after)[0]
-    return reorder(out).reshape((n * x.shape[0],) + x.shape[1:])
+    return reorder(out, lax.axis_index("rows")).reshape((n * x.shape[0],) + x.shape[1:])
 
 
 def scatter_sum(x):
@@ -245,20 +320,39 @@
     return y.reshape((n * x.shape[0],) + x.shape[1:])
 
 
+def sum_rows(x, schur):
+    n = lax.axis_size("rows")
+    if n > 8:
+        total = gather_rows(scatter_sum(x.reshape((n, x.shape[0] // n) + x.shape[1:])))
+        return total, chol_inverse(schur, 0, 1)
+    part = lax.axis_index("rows") // 2
+    half = n // 2
+    deep = x.shape[0] // half
+    x, schur = tie(x + swap(x, 1, "rows"), schur)
+    cuts = [lax.dynamic_slice_in_dim(x, (part ^ k) * deep, deep, 0) for k in range(half)]
+    moved = [swap(cuts[k], 2 * k, "rows") for k in range(1, half)]
+    state = chol_inverse(schur, 0, 1)
+    state, moved[0] = tie(state, moved[0])
+    one = sum(moved, cuts[0])
+    out = jnp.stack([one] + [swap(one, 2 * k, "rows") for k in range(1, half)])
+    return reorder(out, part).reshape(x.shape), state
+
+
 def tie(*xs):
     return lax.optimization_barrier(xs)
 
 
-def gauss(left, right):
+def norms(x):
+    return jnp.sum(x * x, axis=1)
+
+
+def gauss(left, right, ln, rn):
     cross = lax.dot_general(left, right, (((1,), (1,)), ((), ())), precision=NEAR, preferred_element_type=jnp.float32)
-    ln = jnp.sum(left * left, axis=1)
-    rn = jnp.sum(right * right, axis=1)
     dist = ln[:, None] + rn[None, :] - 2.0 * cross
     return jnp.exp(-dist / (2.0 * left.shape[1]))
 
 
-def mul_t(a, b):
-    return lax.dot_general(a, b, (((1,), (1,)), ((), ())), precision=HI, preferred_element_type=jnp.float32)
+CUT = 3
 
 
 def work(points, pivots, targets):
@@ -290,44 +384,53 @@
     two_a = swap(rows_a, 2)
     one_a = swap(rows_a, 1)
     piv_a = jnp.concatenate([rows_a, one_a, two_a, swap(two_a, 1)], axis=1)
-    kern_aa = gauss(piv_a, piv_a)
+    norms_a = norms(piv_a)
+    kern_aa = gauss(piv_a, piv_a, norms_a, norms_a)
     rows_b = gather_places(part_b, kern_aa)
     kern_aa, rows_b = tie(kern_aa, rows_b)
     two_b = swap(rows_b, 2)
     one_b = swap(rows_b, 1)
-    state = chol_inverse(kern_aa, 0, 3)
-    state, two_b, one_b = tie(state, two_b, one_b)
+    goal = jnp.concatenate(goal, axis=0)
+    deep = goals.shape[0]
+
+    own_norms = norms(own)
+
+    def against(pivs, their):
+        kern = gauss(own, pivs, own_norms, their)
+        return kern, lax.dot_general(
+            goal, kern, (((1,), (0,)), ((), ())), precision=HI, preferred_element_type=jnp.float32
+        ).reshape(ncols, deep, block)
+
+    state = chol_inverse(kern_aa, 0, CUT)
+    state, piv_a = tie(state, piv_a)
+    kern_a, sums_a = against(piv_a, norms_a)
+    state, two_b, one_b, sums_a = tie(state, two_b, one_b, sums_a)
     piv_b = jnp.concatenate([rows_b, one_b, two_b, swap(two_b, 1)], axis=1)
-    pivs = jnp.concatenate([piv_a, piv_b], axis=0)
-    kern = gauss(own, pivs)
-    pieces = lax.dot_general(
-        jnp.concatenate(goal, axis=0), kern, (((1,), (0,)), ((), ())), precision=HI, preferred_element_type=jnp.float32
-    ).reshape(ncols, goals.shape[0], kern.shape[1])
-    back = swap(jnp.concatenate([pieces[1], pieces[3]], axis=0), 1)
-    deep = goals.shape[0]
-    home = pieces[0] + back[:deep]
-    away = pieces[2] + back[deep:]
-    side = gauss(tie(piv_b, away)[0], pivs)
+    norms_b = norms(piv_b)
+    kern_b, sums_b = against(piv_b, norms_b)
+
+    def both(k):
+        return jnp.concatenate([sums_a[k], sums_b[k]], axis=1)
+
+    back = swap(jnp.concatenate([both(1), both(3)], axis=0), 1)
+    away = both(2) + back[deep:]
     state, away = tie(state, away)
+    home = both(0) + back[:deep]
     returned = swap(away, 2)
-    inv_one = chol_inverse(state, 3, 4)
-    inv_one, returned = tie(inv_one, returned)
+    inv_one = chol_inverse(state, CUT, 4)
+    side = gauss(
+        tie(piv_b, inv_one)[0], jnp.concatenate([piv_a, piv_b], axis=0), norms_b, jnp.concatenate([norms_a, norms_b])
+    )
+    side, returned = tie(side, returned)
     summed = home + returned
-    summed = scatter_sum(summed.reshape(nrows, deep // nrows, summed.shape[1]))
-    crossed = mul_t(side[:, :block], inv_one)
-    schur = side[:, block:] - mul_t(crossed, crossed)
-    schur, summed = tie(schur, summed)
-    total = gather_rows(summed)
-    inv_two = chol_inverse(schur)
-    own_one = mul_t(kern[:, :block], inv_one)
-    own_left = kern[:, block:] - mul_t(own_one, crossed)
-    inv_two, own_one, own_left, total = tie(inv_two, own_one, own_left, total)
-    tot_one = mul_t(total[:, :block], inv_one)
-    tot_left = total[:, block:] - mul_t(tot_one, crossed)
-    factor = jnp.concatenate([own_one, mul_t(own_left, inv_two)], axis=1)
-    final = jnp.concatenate([tot_one, mul_t(tot_left, inv_two)], axis=1)
-    projection = final.T * (1.0 / math.sqrt(rows_dev * nrows))
-    return (factor, projection)
+    side, _ = tie(side, summed)
+    crossed, schur = schur_of(side, inv_one)
+    total, state = sum_rows(summed, schur)
+    state = chol_inverse(state, 1, 3)
+    factor, projection = finish(
+        1.0 / math.sqrt(rows_dev * nrows), state, kern_a, kern_b, total, inv_one, crossed, 3
+    )
+    return (factor, projection.T)
 
 
 def solution(mesh):

time: 138 us -> 133 us (0.964)
  matrix products: 22.6 us -> 9.11 us
  waiting for transfers between devices: 32.1 us -> 39.1 us
  other arithmetic: 8.89 us -> 2.45 us
  Pallas kernels: 31.8 us -> 36 us
  starting transfers between devices: 36.8 us -> 40.9 us
    ppermute x26 -> x33, starting transfers between devices: 28.8 us -> 40.9 us  [swap(): return lax.ppermute(x, axis, [(i, i ^ mask) for i in range(size)])]
    dot_general x9 -> x2, matrix products: 13.3 us -> 1.23 us  [against(): lax.dot_general(goal, kern, (((1,), (0,)), ((), ())), precision=HI, prefe...]
    pallas_call x0 -> x2, Pallas kernels: none -> 10.8 us  [the longest x1 7.06 us: finish(): pl.pallas_call(functools.partial(finish_kernel, width, sub, first, scale)...]
    ppermute x26 -> x33, waiting for transfers between devices: 30.3 us -> 39.1 us  [swap(): return lax.ppermute(x, axis, [(i, i ^ mask) for i in range(size)])]
    all_to_all x2 -> x0, starting transfers between devices: 7.99 us -> none  [the longest x1 4.27 us: gather_rows(): y = lax.all_to_all(jnp.broadcast_to(x[None], (n,) + x.shape), 'rows', 0, 0)]
    pallas_call x3 -> x4, Pallas kernels: 29.6 us -> 23.1 us  [chol_inverse(): pl.pallas_call(functools.partial(chol_kernel, width, sub, first, last), o...]
    reduce_sum x5 -> x2, other arithmetic: 2.94 us -> 0.36 us  [norms(): return jnp.sum(x * x, axis=1)]
    all_to_all x2 -> x0, waiting for transfers between devices: 1.74 us -> none  [the longest x1 1.74 us: scatter_sum(): return jnp.sum(lax.all_to_all(x, 'rows', 0, 0), axis=0)]
  transfers between devices with their start and end apart: 28 -> 33, of which waited for: 17 -> 15; matrix products, arithmetic and copies ran while one was open for 12% -> 6% of each run, Pallas kernels for 22% -> 18%
where the time goes in v1:
time: 133 us
  starting transfers between devices  40.9 us (31%)
  waiting for transfers between devices  39.1 us (29%)
  Pallas kernels  36 us (27%)
  matrix products  9.11 us (7%)
  local copies, waits for them, and re-layouts  3.99 us (3%)
  other arithmetic  2.45 us (2%)
    ppermute x33, starting transfers between devices, swap(): return lax.ppermute(x, axis, [(i, i ^ mask) for i in range(size)])  40.9 us
    ppermute x33, waiting for transfers between devices, swap(): return lax.ppermute(x, axis, [(i, i ^ mask) for i in range(size)])  39.1 us
    pallas_call x4, Pallas kernels, chol_inverse(): pl.pallas_call(functools.partial(chol_kernel, width, sub, first, last), o...  23.1 us
    dot_general x4, matrix products, gauss(): lax.dot_general(left, right, (((1,), (1,)), ((), ())), precision=NEAR, pr...  7.89 us
    pallas_call x1, Pallas kernels, finish(): pl.pallas_call(functools.partial(finish_kernel, width, sub, first, scale)...  7.06 us
    pallas_call x1, Pallas kernels, schur_of(): pl.pallas_call(schur_kernel, out_shape=(shape, shape), in_specs=[VMEM] *...  3.79 us
  transfers between devices with their start and end apart: 33, of which 15 were waited for; matrix products, arithmetic and copies ran while one was open for 6% of the time, Pallas kernels for 18%

profile of v1, /device:TPU:0, one launch (start us, length us, event | category | flops | bytes accessed | tf_op | source)
XLA Modules:
  0.0 132.8 jit_solution(15189157676166199458)
XLA Ops:
  0.6 1.2 copy-done
  1.9 0.7 copy-done.2
  2.6 2.1 %place.1 = f32[2,8,64,256]{3,2,1,0:T(8,128)S(1)} custom-call(s32[2,512]{1,0:T(2,128)S(1)} %copy-done.2, s32[1]{0:T(128)} %bitcast.me_ref, f32[1024,256]{1,0:T(8,128)S(1)} %copy-done), custom_call_target="tpu_custom_call" | custom-call | flops 1610612736 | bytes 2097152 | tf_op jit(solution)/shard_map/place/pallas_call | solution.py:262
  4.7 0.1 fusion.25
  4.8 0.7 slice_bitcast_fusion.2
  5.5 3.0 %collective-permute-start = (f32[4,64,256]{2,1,0:T(8,128)}, f32[4,64,256]{2,1,0:T(8,128)}, u32[]{:S(2)}, u32[]{:S(2)}) collective-permute-start(f32[4,64,256]{2,1,0:T(8,128)} %slice_bitcast_fusion.2), channel_id=1, source_target_pairs={{0,4},{4,0},{8,12},{12,8},{16,20},{20,16},{24,28},{28,24},{1,5},{5... | collective-permute-start | bytes 786440 | tf_op jit(solution)/shard_map/ppermute | solution.py:275
  8.5 0.1 constant_dynamic-slice_fusion.3
  8.7 1.6 %collective-permute-start.21 = (f32[640,256]{1,0:T(8,128)S(1)}, f32[640,256]{1,0:T(8,128)S(1)}, u32[]{:S(2)}, u32[]{:S(2)}) collective-permute-start(f32[640,256]{1,0:T(8,128)S(1)} %pad_maximum_fusion.2), channel_id=1, source_target_pairs={{0,2},{1,3},{2,0},{3,1},{4,6},{5,7},{6,4},{7,5},{8,10},{9,11},{10,... | collective-permute-start | bytes 1966088 | tf_op jit(solution)/shard_map/ppermute | solution.py:275
  10.3 0.6 collective-permute-start.11
  10.9 5.1 %collective-permute-done = f32[4,64,256]{2,1,0:T(8,128)} collective-permute-done((f32[4,64,256]{2,1,0:T(8,128)}, f32[4,64,256]{2,1,0:T(8,128)}, u32[]{:S(2)}, u32[]{:S(2)}) %collective-permute-start) | collective-permute-done | bytes 262176 | tf_op jit(solution)/shard_map/ppermute | solution.py:275
  16.0 1.0 fusion.7
  17.0 2.1 %collective-permute-start.1 = (f32[64,256]{1,0:T(8,128)S(1)}, f32[64,256]{1,0:T(8,128)S(1)}, u32[]{:S(2)}, u32[]{:S(2)}) collective-permute-start(f32[64,256]{1,0:T(8,128)S(1)} %get-tuple-element.84), channel_id=1, source_target_pairs={{0,8},{4,12},{8,0},{12,4},{16,24},{20,28},{24,16},{28,20},{1,9},{5... | collective-permute-start | bytes 196616 | tf_op jit(solution)/shard_map/ppermute | solution.py:275
  19.2 2.6 %collective-permute-start.2 = (f32[64,256]{1,0:T(8,128)S(1)}, f32[64,256]{1,0:T(8,128)S(1)}, u32[]{:S(2)}, u32[]{:S(2)}) collective-permute-start(f32[64,256]{1,0:T(8,128)S(1)} %get-tuple-element.86), channel_id=1, source_target_pairs={{0,16},{4,20},{8,24},{12,28},{16,0},{20,4},{24,8},{28,12},{1,17},{... | collective-permute-start | bytes 196616 | tf_op jit(solution)/shard_map/ppermute | solution.py:275
  21.8 1.0 collective-permute-start.12
  22.8 2.7 %collective-permute-done.2 = f32[64,256]{1,0:T(8,128)S(1)} collective-permute-done((f32[64,256]{1,0:T(8,128)S(1)}, f32[64,256]{1,0:T(8,128)S(1)}, u32[]{:S(2)}, u32[]{:S(2)}) %collective-permute-start.2) | collective-permute-done | bytes 65568 | tf_op jit(solution)/shard_map/ppermute | solution.py:275
  25.5 2.3 %collective-permute-done.3 = f32[64,256]{1,0:T(8,128)S(1)} collective-permute-done((f32[64,256]{1,0:T(8,128)S(1)}, f32[64,256]{1,0:T(8,128)S(1)}, u32[]{:S(2)}, u32[]{:S(2)}) %collective-permute-start.3) | collective-permute-done | bytes 65568 | tf_op jit(solution)/shard_map/ppermute | solution.py:275
  27.9 0.2 collective-permute-start.5
  28.1 1.3 collective-permute-start.6
  29.4 2.1 %collective-permute-start.4 = (f32[64,256]{1,0:T(8,128)S(1)}, f32[64,256]{1,0:T(8,128)S(1)}, u32[]{:S(2)}, u32[]{:S(2)}) collective-permute-start(f32[64,256]{1,0:T(8,128)S(1)} %fusion.15), channel_id=1, source_target_pairs={{0,8},{4,12},{8,0},{12,4},{16,24},{20,28},{24,16},{28,20},{1,9},{5... | collective-permute-start | bytes 196616 | tf_op jit(solution)/shard_map/ppermute | solution.py:275
  31.4 1.0 collective-permute-start.13
  32.5 2.7 %collective-permute-done.5 = f32[64,256]{1,0:T(8,128)S(1)} collective-permute-done((f32[64,256]{1,0:T(8,128)S(1)}, f32[64,256]{1,0:T(8,128)S(1)}, u32[]{:S(2)}, u32[]{:S(2)}) %collective-permute-start.5) | collective-permute-done | bytes 65568 | tf_op jit(solution)/shard_map/ppermute | solution.py:275
  35.2 2.1 %collective-permute-start.14 = (f32[64,256]{1,0:T(8,128)S(1)}, f32[64,256]{1,0:T(8,128)S(1)}, u32[]{:S(2)}, u32[]{:S(2)}) collective-permute-start(f32[64,256]{1,0:T(8,128)S(1)} %get-tuple-element.80), channel_id=1, source_target_pairs={{0,24},{4,28},{8,16},{12,20},{16,8},{20,12},{24,0},{28,4},{1,25},{... | collective-permute-start | bytes 196616 | tf_op jit(solution)/shard_map/ppermute | solution.py:275
  37.4 1.6 %collective-permute-start.7 = (f32[4,64,256]{2,1,0:T(8,128)S(1)}, f32[4,64,256]{2,1,0:T(8,128)S(1)}, u32[]{:S(2)}, u32[]{:S(2)}) collective-permute-start(f32[4,64,256]{2,1,0:T(8,128)S(1)} %get-tuple-element.83), channel_id=1, source_target_pairs={{0,4},{4,0},{8,12},{12,8},{16,20},{20,16},{24,28},{28,24},{1,5},{5... | collective-permute-start | bytes 786440 | tf_op jit(solution)/shard_map/ppermute | solution.py:275
  39.0 3.1 %collective-permute-done.14 = f32[64,256]{1,0:T(8,128)S(1)} collective-permute-done((f32[64,256]{1,0:T(8,128)S(1)}, f32[64,256]{1,0:T(8,128)S(1)}, u32[]{:S(2)}, u32[]{:S(2)}) %collective-permute-start.14) | collective-permute-done | bytes 65568 | tf_op jit(solution)/shard_map/ppermute | solution.py:275
  42.1 0.1 collective-permute-start.15
  42.2 2.5 %collective-permute-start.16 = (f32[64,256]{1,0:T(8,128)S(1)}, f32[64,256]{1,0:T(8,128)S(1)}, u32[]{:S(2)}, u32[]{:S(2)}) collective-permute-start(f32[64,256]{1,0:T(8,128)S(1)} %fusion.12), channel_id=1, source_target_pairs={{0,16},{4,20},{8,24},{12,28},{16,0},{20,4},{24,8},{28,12},{1,17},{... | collective-permute-start | bytes 196616 | tf_op jit(solution)/shard_map/ppermute | solution.py:275
  44.7 1.8 %collective-permute-start.17 = (f32[64,256]{1,0:T(8,128)S(1)}, f32[64,256]{1,0:T(8,128)S(1)}, u32[]{:S(2)}, u32[]{:S(2)}) collective-permute-start(f32[64,256]{1,0:T(8,128)S(1)} %fusion.12), channel_id=1, source_target_pairs={{0,24},{4,28},{8,16},{12,20},{16,8},{20,12},{24,0},{28,4},{1,25},{... | collective-permute-start | bytes 196616 | tf_op jit(solution)/shard_map/ppermute | solution.py:275
  46.9 1.6 %collective-permute-start.9 = (f32[512,256]{1,0:T(8,128)S(1)}, f32[512,256]{1,0:T(8,128)S(1)}, u32[]{:S(2)}, u32[]{:S(2)}) collective-permute-start(f32[512,256]{1,0:T(8,128)S(1)} %bitcast.124), channel_id=1, source_target_pairs={{0,2},{1,3},{2,0},{3,1},{4,6},{5,7},{6,4},{7,5},{8,10},{9,11},{10,... | collective-permute-start | bytes 1572872 | tf_op jit(solution)/shard_map/ppermute | solution.py:275
  48.5 2.3 %collective-permute-done.17 = f32[64,256]{1,0:T(8,128)S(1)} collective-permute-done((f32[64,256]{1,0:T(8,128)S(1)}, f32[64,256]{1,0:T(8,128)S(1)}, u32[]{:S(2)}, u32[]{:S(2)}) %collective-permute-start.17) | collective-permute-done | bytes 65568 | tf_op jit(solution)/shard_map/ppermute | solution.py:275
  50.8 1.6 %collective-permute-start.18 = (f32[4,64,256]{2,1,0:T(8,128)S(1)}, f32[4,64,256]{2,1,0:T(8,128)S(1)}, u32[]{:S(2)}, u32[]{:S(2)}) collective-permute-start(f32[4,64,256]{2,1,0:T(8,128)S(1)} %get-tuple-element.78), channel_id=1, source_target_pairs={{0,4},{4,0},{8,12},{12,8},{16,20},{20,16},{24,28},{28,24},{1,5},{5... | collective-permute-start | bytes 786440 | tf_op jit(solution)/shard_map/ppermute | solution.py:275
  52.5 4.8 %collective-permute-done.18 = f32[4,64,256]{2,1,0:T(8,128)S(1)} collective-permute-done((f32[4,64,256]{2,1,0:T(8,128)S(1)}, f32[4,64,256]{2,1,0:T(8,128)S(1)}, u32[]{:S(2)}, u32[]{:S(2)}) %collective-permute-start.18) | collective-permute-done | bytes 262176 | tf_op jit(solution)/shard_map/ppermute | solution.py:275
  57.3 4.0 %collective-permute-done.9 = f32[512,256]{1,0:T(8,128)S(1)} collective-permute-done((f32[512,256]{1,0:T(8,128)S(1)}, f32[512,256]{1,0:T(8,128)S(1)}, u32[]{:S(2)}, u32[]{:S(2)}) %collective-permute-start.9) | collective-permute-done | bytes 524320 | tf_op jit(solution)/shard_map/ppermute | solution.py:275
  61.4 0.1 multiply_reduce_fusion.2
  61.5 1.7 %collective-permute-done.10 = f32[512,256]{1,0:T(8,128)S(1)} collective-permute-done((f32[512,256]{1,0:T(8,128)S(1)}, f32[512,256]{1,0:T(8,128)S(1)}, u32[]{:S(2)}, u32[]{:S(2)}) %collective-permute-start.10) | collective-permute-done | bytes 524320 | tf_op jit(solution)/shard_map/ppermute | solution.py:275
  63.2 0.3 pad_maximum_fusion
  63.5 1.9 %multiply_exponential_fusion.1.a_ref = f32[512,512]{1,0:T(8,128)S(1)} fusion(f32[512]{0:T(512)S(1)} %get-tuple-element.51, f32[512,256]{1,0:T(8,128)S(1)} %collective-permute-done.10, f32[512,256]{1,0:T(8,128)S(1)} %collective-permute-done.9, f32[512,256]{1,0:T(8,128)S(1)} %collective-permute-done.8, f32[512,256]{1,0:T(8,128)S(1)} %bitcast.127), kind=kOutput, calls=%fused_computation.13 | convolution fusion | flops 1613496320 | bytes 3147776 | tf_op jit(solution)/shard_map/dot_general | solution.py:350
  65.6 1.6 %collective-permute-start.19 = (f32[512,256]{1,0:T(8,128)S(1)}, f32[512,256]{1,0:T(8,128)S(1)}, u32[]{:S(2)}, u32[]{:S(2)}) collective-permute-start(f32[512,256]{1,0:T(8,128)S(1)} %bitcast.115), channel_id=1, source_target_pairs={{0,2},{1,3},{2,0},{3,1},{4,6},{5,7},{6,4},{7,5},{8,10},{9,11},{10,... | collective-permute-start | bytes 1572872 | tf_op jit(solution)/shard_map/ppermute | solution.py:275
  67.2 10.4 %chol.4.a_ref = f32[512,512]{1,0:T(8,128)S(1)} custom-call(f32[512,512]{1,0:T(8,128)S(1)} %multiply_exponential_fusion.1.a_ref), custom_call_target="tpu_custom_call", output_to_operand_aliasing={{}: (0, {})} | custom-call | flops 9663676416 | bytes 2097152 | tf_op jit(solution)/shard_map/chol/pallas_call | solution.py:164
  77.6 1.1 multiply_exponential_fusion.3.k1_ref
  78.7 0.6 fusion.9
  79.3 0.4 collective-permute-done.19
  79.7 0.2 collective-permute-start.23
  80.1 1.4 %collective-permute-done.23 = f32[512,256]{1,0:T(8,128)S(1)} collective-permute-done((f32[512,256]{1,0:T(8,128)S(1)}, f32[512,256]{1,0:T(8,128)S(1)}, u32[]{:S(2)}, u32[]{:S(2)}) %collective-permute-start.23) | collective-permute-done | bytes 524320 | tf_op jit(solution)/shard_map/ppermute | solution.py:275
  81.6 0.2 multiply_reduce_fusion
  81.9 1.2 multiply_exponential_fusion.2.k2_ref
  83.1 0.6 fusion.8
  83.7 0.7 fusion.28
  84.4 0.3 collective-permute-start.24
  84.7 1.7 %collective-permute-done.24 = f32[128,1024]{1,0:T(8,128)S(1)} collective-permute-done((f32[128,1024]{1,0:T(8,128)S(1)}, f32[128,1024]{1,0:T(8,128)S(1)}, u32[]{:S(2)}, u32[]{:S(2)}) %collective-permute-start.24) | collective-permute-done | bytes 524320 | tf_op jit(solution)/shard_map/ppermute | solution.py:275
  86.5 2.7 %chol.5.one_ref = f32[512,512]{1,0:T(8,128)S(1)} custom-call(f32[512,512]{1,0:T(8,128)S(1)} %chol.4.a_ref), custom_call_target="tpu_custom_call", output_to_operand_aliasing={{}: (0, {})} | custom-call | flops 3221225472 | bytes 2097152 | tf_op jit(solution)/shard_map/chol/pallas_call | solution.py:164
  89.2 1.6 %collective-permute-start.25 = (f32[64,1024]{1,0:T(8,128)S(1)}, f32[64,1024]{1,0:T(8,128)S(1)}, u32[]{:S(2)}, u32[]{:S(2)}) collective-permute-start(f32[64,1024]{1,0:T(8,128)S(1)} %slice_add_fusion), channel_id=1, source_target_pairs={{0,2},{1,3},{2,0},{3,1},{4,6},{5,7},{6,4},{7,5},{8,10},{9,11},{10,... | collective-permute-start | bytes 786440 | tf_op jit(solution)/shard_map/ppermute | solution.py:275
  90.8 3.6 %multiply_exponential_fusion.side_ref = f32[512,1024]{1,0:T(8,128)S(1)} fusion(f32[1024]{0:T(1024)S(1)} %pad_maximum_fusion.16, f32[512]{0:T(512)S(1)} %multiply_reduce_fusion, f32[512,1024]{1,0:T(8,128)S(1)} %copy-done.4, f32[512,1024]{1,0:T(8,128)S(1)} %copy-done.6), kind=kOutput, calls=%fused_computation.5 | convolution fusion | flops 3224895488 | bytes 6297600 | tf_op jit(solution)/shard_map/dot_general | solution.py:350
  94.4 3.3 %collective-permute-done.25 = f32[64,1024]{1,0:T(8,128)S(1)} collective-permute-done((f32[64,1024]{1,0:T(8,128)S(1)}, f32[64,1024]{1,0:T(8,128)S(1)}, u32[]{:S(2)}, u32[]{:S(2)}) %collective-permute-start.25) | collective-permute-done | bytes 262176 | tf_op jit(solution)/shard_map/ppermute | solution.py:275
  97.7 1.6 %collective-permute-start.26 = (f32[64,1024]{1,0:T(8,128)S(1)}, f32[64,1024]{1,0:T(8,128)S(1)}, u32[]{:S(2)}, u32[]{:S(2)}) collective-permute-start(f32[64,1024]{1,0:T(8,128)S(1)} %fusion.5), channel_id=1, source_target_pairs={{0,4},{4,0},{8,12},{12,8},{16,20},{20,16},{24,28},{28,24},{1,5},{5... | collective-permute-start | bytes 786440 | tf_op jit(solution)/shard_map/ppermute | solution.py:275
  99.3 3.8 %schur.1 = (f32[512,512]{1,0:T(8,128)S(1)}, f32[512,512]{1,0:T(8,128)S(1)}) custom-call(f32[512,1024]{1,0:T(8,128)S(1)} %multiply_exponential_fusion.side_ref, f32[512,512]{1,0:T(8,128)S(1)} %chol.5.one_ref), custom_call_target="tpu_custom_call" | custom-call | flops 3221225472 | bytes 5242880 | tf_op jit(solution)/shard_map/schur/pallas_call | solution.py:187
  103.1 2.2 %collective-permute-done.26 = f32[64,1024]{1,0:T(8,128)S(1)} collective-permute-done((f32[64,1024]{1,0:T(8,128)S(1)}, f32[64,1024]{1,0:T(8,128)S(1)}, u32[]{:S(2)}, u32[]{:S(2)}) %collective-permute-start.26) | collective-permute-done | bytes 262176 | tf_op jit(solution)/shard_map/ppermute | solution.py:275
  105.5 2.5 %collective-permute-start.28 = (f32[16,1024]{1,0:T(8,128)S(1)}, f32[16,1024]{1,0:T(8,128)S(1)}, u32[]{:S(2)}, u32[]{:S(2)}) collective-permute-start(f32[16,1024]{1,0:T(8,128)S(1)} %get-tuple-element.70), channel_id=1, source_target_pairs={{0,16},{4,20},{8,24},{12,28},{16,0},{20,4},{24,8},{28,12},{1,17},{... | collective-permute-start | bytes 196616 | tf_op jit(solution)/shard_map/ppermute | solution.py:275
  108.0 1.9 %collective-permute-start.29 = (f32[16,1024]{1,0:T(8,128)S(1)}, f32[16,1024]{1,0:T(8,128)S(1)}, u32[]{:S(2)}, u32[]{:S(2)}) collective-permute-start(f32[16,1024]{1,0:T(8,128)S(1)} %get-tuple-element.71), channel_id=1, source_target_pairs={{0,24},{4,28},{8,16},{12,20},{16,8},{20,12},{24,0},{28,4},{1,25},{... | collective-permute-start | bytes 196616 | tf_op jit(solution)/shard_map/ppermute | solution.py:275
  109.9 3.2 %chol.6.a_ref = f32[512,512]{1,0:T(8,128)S(1)} custom-call(f32[512,512]{1,0:T(8,128)S(1)} %get-tuple-element.43.a_ref), custom_call_target="tpu_custom_call", output_to_operand_aliasing={{}: (0, {})} | custom-call | flops 3221225472 | bytes 2097152 | tf_op jit(solution)/shard_map/chol/pallas_call | solution.py:164
  113.1 1.2 collective-permute-done.29
  114.4 2.4 %collective-permute-start.31 = (f32[16,1024]{1,0:T(8,128)S(1)}, f32[16,1024]{1,0:T(8,128)S(1)}, u32[]{:S(2)}, u32[]{:S(2)}) collective-permute-start(f32[16,1024]{1,0:T(8,128)S(1)} %add_add_fusion), channel_id=1, source_target_pairs={{0,16},{4,20},{8,24},{12,28},{16,0},{20,4},{24,8},{28,12},{1,17},{... | collective-permute-start | bytes 196616 | tf_op jit(solution)/shard_map/ppermute | solution.py:275
  116.9 1.9 %collective-permute-start.32 = (f32[16,1024]{1,0:T(8,128)S(1)}, f32[16,1024]{1,0:T(8,128)S(1)}, u32[]{:S(2)}, u32[]{:S(2)}) collective-permute-start(f32[16,1024]{1,0:T(8,128)S(1)} %add_add_fusion), channel_id=1, source_target_pairs={{0,24},{4,28},{8,16},{12,20},{16,8},{20,12},{24,0},{28,4},{1,25},{... | collective-permute-start | bytes 196616 | tf_op jit(solution)/shard_map/ppermute | solution.py:275
  118.8 6.8 %chol.7.a_ref = f32[512,512]{1,0:T(8,128)S(1)} custom-call(f32[512,512]{1,0:T(8,128)S(1)} %chol.6.a_ref), custom_call_target="tpu_custom_call", output_to_operand_aliasing={{}: (0, {})} | custom-call | flops 6442450944 | bytes 2097152 | tf_op jit(solution)/shard_map/chol/pallas_call | solution.py:164
  125.7 7.1 %finish.1 = (f32[256,1024]{1,0:T(8,128)}, f32[64,1024]{1,0:T(8,128)}, f32[512,512]{1,0:T(8,128)S(1)}) custom-call(f32[512,512]{1,0:T(8,128)S(1)} %chol.7.a_ref, f32[256,512]{1,0:T(8,128)S(1)} %multiply_exponential_fusion.3.k1_ref, f32[256,512]{1,0:T(8,128)S(1)} %multiply_exponential_fusion.2.k2_ref, ...), custom_call_target="tpu_custom_call", output_to_operand_aliasing={{2}: (0, {})} | custom-call | flops 1509949440 | bytes 4194304 | tf_op jit(solution)/shard_map/finish/pallas_call | solution.py:220
  (80 shorter events, 1.6 us)
Async XLA Ops:
  0.6 1.2 copy-start
  1.9 0.7 copy-start.2
  4.7 3.9 %copy-start.1 = (f32[1024,256]{1,0:T(8,128)S(1)}, f32[1024,256]{1,0:T(8,128)}, u32[]{:S(2)}) copy-start(f32[1024,256]{1,0:T(8,128)} %pts_ref.1) | copy-start | bytes 3145732
  4.7 3.9 %copy-start.8 = (f32[1024,64]{0,1:T(8,128)S(1)}, f32[1024,64]{0,1:T(8,128)}, u32[]{:S(2)}) copy-start(f32[1024,64]{0,1:T(8,128)} %param.5) | copy-start | bytes 786436
  5.5 10.5 %collective-permute-start = (f32[4,64,256]{2,1,0:T(8,128)}, f32[4,64,256]{2,1,0:T(8,128)}, u32[]{:S(2)}, u32[]{:S(2)}) collective-permute-start(f32[4,64,256]{2,1,0:T(8,128)} %slice_bitcast_fusion.2), channel_id=1, source_target_pairs={{0,4},{4,0},{8,12},{12,8},{16,20},{20,16},{24,28},{28,24},{1,5},{5... | collective-permute-start | bytes 786440 | tf_op jit(solution)/shard_map/ppermute | solution.py:275
  8.7 37.8 %collective-permute-start.21 = (f32[640,256]{1,0:T(8,128)S(1)}, f32[640,256]{1,0:T(8,128)S(1)}, u32[]{:S(2)}, u32[]{:S(2)}) collective-permute-start(f32[640,256]{1,0:T(8,128)S(1)} %pad_maximum_fusion.2), channel_id=1, source_target_pairs={{0,2},{1,3},{2,0},{3,1},{4,6},{5,7},{6,4},{7,5},{8,10},{9,11},{10,... | collective-permute-start | bytes 1966088 | tf_op jit(solution)/shard_map/ppermute | solution.py:275
  10.3 11.5 %collective-permute-start.11 = (f32[4,64,256]{2,1,0:T(8,128)S(1)}, f32[4,64,256]{2,1,0:T(8,128)S(1)}, u32[]{:S(2)}, u32[]{:S(2)}) collective-permute-start(f32[4,64,256]{2,1,0:T(8,128)S(1)} %slice_bitcast_fusion), channel_id=1, source_target_pairs={{0,4},{4,0},{8,12},{12,8},{16,20},{20,16},{24,28},{28,24},{1,5},{5... | collective-permute-start | bytes 786440 | tf_op jit(solution)/shard_map/ppermute | solution.py:275
  17.0 5.8 %collective-permute-start.1 = (f32[64,256]{1,0:T(8,128)S(1)}, f32[64,256]{1,0:T(8,128)S(1)}, u32[]{:S(2)}, u32[]{:S(2)}) collective-permute-start(f32[64,256]{1,0:T(8,128)S(1)} %get-tuple-element.84), channel_id=1, source_target_pairs={{0,8},{4,12},{8,0},{12,4},{16,24},{20,28},{24,16},{28,20},{1,9},{5... | collective-permute-start | bytes 196616 | tf_op jit(solution)/shard_map/ppermute | solution.py:275
  19.2 6.4 %collective-permute-start.2 = (f32[64,256]{1,0:T(8,128)S(1)}, f32[64,256]{1,0:T(8,128)S(1)}, u32[]{:S(2)}, u32[]{:S(2)}) collective-permute-start(f32[64,256]{1,0:T(8,128)S(1)} %get-tuple-element.86), channel_id=1, source_target_pairs={{0,16},{4,20},{8,24},{12,28},{16,0},{20,4},{24,8},{28,12},{1,17},{... | collective-permute-start | bytes 196616 | tf_op jit(solution)/shard_map/ppermute | solution.py:275
  21.8 6.1 %collective-permute-start.3 = (f32[64,256]{1,0:T(8,128)S(1)}, f32[64,256]{1,0:T(8,128)S(1)}, u32[]{:S(2)}, u32[]{:S(2)}) collective-permute-start(f32[64,256]{1,0:T(8,128)S(1)} %get-tuple-element.85), channel_id=1, source_target_pairs={{0,24},{4,28},{8,16},{12,20},{16,8},{20,12},{24,0},{28,4},{1,25},{... | collective-permute-start | bytes 196616 | tf_op jit(solution)/shard_map/ppermute | solution.py:275
  21.8 9.6 %collective-permute-start.12 = (f32[64,256]{1,0:T(8,128)S(1)}, f32[64,256]{1,0:T(8,128)S(1)}, u32[]{:S(2)}, u32[]{:S(2)}) collective-permute-start(f32[64,256]{1,0:T(8,128)S(1)} %get-tuple-element.79), channel_id=1, source_target_pairs={{0,8},{4,12},{8,0},{12,4},{16,24},{20,28},{24,16},{28,20},{1,9},{5... | collective-permute-start | bytes 196616 | tf_op jit(solution)/shard_map/ppermute | solution.py:275
  27.9 7.3 %collective-permute-start.5 = (f32[64,256]{1,0:T(8,128)S(1)}, f32[64,256]{1,0:T(8,128)S(1)}, u32[]{:S(2)}, u32[]{:S(2)}) collective-permute-start(f32[64,256]{1,0:T(8,128)S(1)} %fusion.15), channel_id=1, source_target_pairs={{0,16},{4,20},{8,24},{12,28},{16,0},{20,4},{24,8},{28,12},{1,17},{... | collective-permute-start | bytes 196616 | tf_op jit(solution)/shard_map/ppermute | solution.py:275
  28.1 9.2 %collective-permute-start.6 = (f32[64,256]{1,0:T(8,128)S(1)}, f32[64,256]{1,0:T(8,128)S(1)}, u32[]{:S(2)}, u32[]{:S(2)}) collective-permute-start(f32[64,256]{1,0:T(8,128)S(1)} %fusion.15), channel_id=1, source_target_pairs={{0,24},{4,28},{8,16},{12,20},{16,8},{20,12},{24,0},{28,4},{1,25},{... | collective-permute-start | bytes 196616 | tf_op jit(solution)/shard_map/ppermute | solution.py:275
  29.4 8.0 %collective-permute-start.4 = (f32[64,256]{1,0:T(8,128)S(1)}, f32[64,256]{1,0:T(8,128)S(1)}, u32[]{:S(2)}, u32[]{:S(2)}) collective-permute-start(f32[64,256]{1,0:T(8,128)S(1)} %fusion.15), channel_id=1, source_target_pairs={{0,8},{4,12},{8,0},{12,4},{16,24},{20,28},{24,16},{28,20},{1,9},{5... | collective-permute-start | bytes 196616 | tf_op jit(solution)/shard_map/ppermute | solution.py:275
  31.4 7.5 %collective-permute-start.13 = (f32[64,256]{1,0:T(8,128)S(1)}, f32[64,256]{1,0:T(8,128)S(1)}, u32[]{:S(2)}, u32[]{:S(2)}) collective-permute-start(f32[64,256]{1,0:T(8,128)S(1)} %get-tuple-element.81), channel_id=1, source_target_pairs={{0,16},{4,20},{8,24},{12,28},{16,0},{20,4},{24,8},{28,12},{1,17},{... | collective-permute-start | bytes 196616 | tf_op jit(solution)/shard_map/ppermute | solution.py:275
  35.2 6.9 %collective-permute-start.14 = (f32[64,256]{1,0:T(8,128)S(1)}, f32[64,256]{1,0:T(8,128)S(1)}, u32[]{:S(2)}, u32[]{:S(2)}) collective-permute-start(f32[64,256]{1,0:T(8,128)S(1)} %get-tuple-element.80), channel_id=1, source_target_pairs={{0,24},{4,28},{8,16},{12,20},{16,8},{20,12},{24,0},{28,4},{1,25},{... | collective-permute-start | bytes 196616 | tf_op jit(solution)/shard_map/ppermute | solution.py:275
  37.4 9.4 %collective-permute-start.7 = (f32[4,64,256]{2,1,0:T(8,128)S(1)}, f32[4,64,256]{2,1,0:T(8,128)S(1)}, u32[]{:S(2)}, u32[]{:S(2)}) collective-permute-start(f32[4,64,256]{2,1,0:T(8,128)S(1)} %get-tuple-element.83), channel_id=1, source_target_pairs={{0,4},{4,0},{8,12},{12,8},{16,20},{20,16},{24,28},{28,24},{1,5},{5... | collective-permute-start | bytes 786440 | tf_op jit(solution)/shard_map/ppermute | solution.py:275
  42.1 6.4 %collective-permute-start.15 = (f32[64,256]{1,0:T(8,128)S(1)}, f32[64,256]{1,0:T(8,128)S(1)}, u32[]{:S(2)}, u32[]{:S(2)}) collective-permute-start(f32[64,256]{1,0:T(8,128)S(1)} %fusion.12), channel_id=1, source_target_pairs={{0,8},{4,12},{8,0},{12,4},{16,24},{20,28},{24,16},{28,20},{1,9},{5... | collective-permute-start | bytes 196616 | tf_op jit(solution)/shard_map/ppermute | solution.py:275
  42.2 6.3 %collective-permute-start.16 = (f32[64,256]{1,0:T(8,128)S(1)}, f32[64,256]{1,0:T(8,128)S(1)}, u32[]{:S(2)}, u32[]{:S(2)}) collective-permute-start(f32[64,256]{1,0:T(8,128)S(1)} %fusion.12), channel_id=1, source_target_pairs={{0,16},{4,20},{8,24},{12,28},{16,0},{20,4},{24,8},{28,12},{1,17},{... | collective-permute-start | bytes 196616 | tf_op jit(solution)/shard_map/ppermute | solution.py:275
  44.7 6.1 %collective-permute-start.17 = (f32[64,256]{1,0:T(8,128)S(1)}, f32[64,256]{1,0:T(8,128)S(1)}, u32[]{:S(2)}, u32[]{:S(2)}) collective-permute-start(f32[64,256]{1,0:T(8,128)S(1)} %fusion.12), channel_id=1, source_target_pairs={{0,24},{4,28},{8,16},{12,20},{16,8},{20,12},{24,0},{28,4},{1,25},{... | collective-permute-start | bytes 196616 | tf_op jit(solution)/shard_map/ppermute | solution.py:275
  46.6 14.7 %collective-permute-start.22 = (f32[640,256]{1,0:T(8,128)S(1)}, f32[640,256]{1,0:T(8,128)S(1)}, u32[]{:S(2)}, u32[]{:S(2)}) collective-permute-start(f32[640,256]{1,0:T(8,128)S(1)} %pad_maximum_fusion.3), channel_id=1, source_target_pairs={{0,1},{1,0},{2,3},{3,2},{4,5},{5,4},{6,7},{7,6},{8,9},{9,8},{10,11... | collective-permute-start | bytes 1966088 | tf_op jit(solution)/shard_map/ppermute | solution.py:275
  46.9 14.4 %collective-permute-start.9 = (f32[512,256]{1,0:T(8,128)S(1)}, f32[512,256]{1,0:T(8,128)S(1)}, u32[]{:S(2)}, u32[]{:S(2)}) collective-permute-start(f32[512,256]{1,0:T(8,128)S(1)} %bitcast.124), channel_id=1, source_target_pairs={{0,2},{1,3},{2,0},{3,1},{4,6},{5,7},{6,4},{7,5},{8,10},{9,11},{10,... | collective-permute-start | bytes 1572872 | tf_op jit(solution)/shard_map/ppermute | solution.py:275
  50.8 6.4 %collective-permute-start.18 = (f32[4,64,256]{2,1,0:T(8,128)S(1)}, f32[4,64,256]{2,1,0:T(8,128)S(1)}, u32[]{:S(2)}, u32[]{:S(2)}) collective-permute-start(f32[4,64,256]{2,1,0:T(8,128)S(1)} %get-tuple-element.78), channel_id=1, source_target_pairs={{0,4},{4,0},{8,12},{12,8},{16,20},{20,16},{24,28},{28,24},{1,5},{5... | collective-permute-start | bytes 786440 | tf_op jit(solution)/shard_map/ppermute | solution.py:275
  52.4 9.1 %collective-permute-start.8 = (f32[512,256]{1,0:T(8,128)S(1)}, f32[512,256]{1,0:T(8,128)S(1)}, u32[]{:S(2)}, u32[]{:S(2)}) collective-permute-start(f32[512,256]{1,0:T(8,128)S(1)} %bitcast.125), channel_id=1, source_target_pairs={{0,1},{1,0},{2,3},{3,2},{4,5},{5,4},{6,7},{7,6},{8,9},{9,8},{10,11... | collective-permute-start | bytes 1572872 | tf_op jit(solution)/shard_map/ppermute | solution.py:275
  61.3 1.9 %collective-permute-start.10 = (f32[512,256]{1,0:T(8,128)S(1)}, f32[512,256]{1,0:T(8,128)S(1)}, u32[]{:S(2)}, u32[]{:S(2)}) collective-permute-start(f32[512,256]{1,0:T(8,128)S(1)} %collective-permute-done.9), channel_id=1, source_target_pairs={{0,1},{1,0},{2,3},{3,2},{4,5},{5,4},{6,7},{7,6},{8,9},{9,8},{10,11... | collective-permute-start | bytes 1572872 | tf_op jit(solution)/shard_map/ppermute | solution.py:275
  63.5 14.0 %copy-start.5 = (f32[512,1024]{1,0:T(8,128)}, f32[512,1024]{1,0:T(8,128)S(1)}, u32[]{:S(2)}) copy-start(f32[512,1024]{1,0:T(8,128)S(1)} %get-tuple-element.31) | copy-start | bytes 6291460
  65.6 14.0 %collective-permute-start.19 = (f32[512,256]{1,0:T(8,128)S(1)}, f32[512,256]{1,0:T(8,128)S(1)}, u32[]{:S(2)}, u32[]{:S(2)}) collective-permute-start(f32[512,256]{1,0:T(8,128)S(1)} %bitcast.115), channel_id=1, source_target_pairs={{0,2},{1,3},{2,0},{3,1},{4,6},{5,7},{6,4},{7,5},{8,10},{9,11},{10,... | collective-permute-start | bytes 1572872 | tf_op jit(solution)/shard_map/ppermute | solution.py:275
  67.2 12.5 %collective-permute-start.20 = (f32[512,256]{1,0:T(8,128)S(1)}, f32[512,256]{1,0:T(8,128)S(1)}, u32[]{:S(2)}, u32[]{:S(2)}) collective-permute-start(f32[512,256]{1,0:T(8,128)S(1)} %bitcast.116), channel_id=1, source_target_pairs={{0,1},{1,0},{2,3},{3,2},{4,5},{5,4},{6,7},{7,6},{8,9},{9,8},{10,11... | collective-permute-start | bytes 1572872 | tf_op jit(solution)/shard_map/ppermute | solution.py:275
  79.7 1.9 %collective-permute-start.23 = (f32[512,256]{1,0:T(8,128)S(1)}, f32[512,256]{1,0:T(8,128)S(1)}, u32[]{:S(2)}, u32[]{:S(2)}) collective-permute-start(f32[512,256]{1,0:T(8,128)S(1)} %collective-permute-done.19), channel_id=1, source_target_pairs={{0,1},{1,0},{2,3},{3,2},{4,5},{5,4},{6,7},{7,6},{8,9},{9,8},{10,11... | collective-permute-start | bytes 1572872 | tf_op jit(solution)/shard_map/ppermute | solution.py:275
  81.6 1.4 %copy-start.3 = (f32[512,1024]{1,0:T(8,128)}, f32[512,1024]{1,0:T(8,128)S(1)}, u32[]{:S(2)}) copy-start(f32[512,1024]{1,0:T(8,128)S(1)} %constant_dynamic-update-slice_fusion) | copy-start | bytes 6291460
  84.4 2.0 %collective-permute-start.24 = (f32[128,1024]{1,0:T(8,128)S(1)}, f32[128,1024]{1,0:T(8,128)S(1)}, u32[]{:S(2)}, u32[]{:S(2)}) collective-permute-start(f32[128,1024]{1,0:T(8,128)S(1)} %maximum_maximum_fusion), channel_id=1, source_target_pairs={{0,1},{1,0},{2,3},{3,2},{4,5},{5,4},{6,7},{7,6},{8,9},{9,8},{10,11... | collective-permute-start | bytes 1572872 | tf_op jit(solution)/shard_map/ppermute | solution.py:275
  86.4 4.3 %copy-start.4 = (f32[512,1024]{1,0:T(8,128)S(1)}, f32[512,1024]{1,0:T(8,128)}, u32[]{:S(2)}) copy-start(f32[512,1024]{1,0:T(8,128)} %copy-done.3) | copy-start | bytes 6291460
  86.5 4.3 %copy-start.6 = (f32[512,1024]{1,0:T(8,128)S(1)}, f32[512,1024]{1,0:T(8,128)}, u32[]{:S(2)}) copy-start(f32[512,1024]{1,0:T(8,128)} %copy-done.5) | copy-start | bytes 6291460
  89.2 8.5 %copy-start.7 = (f32[64,512]{1,0:T(8,128)S(1)}, f32[64,512]{1,0:T(8,128)}, u32[]{:S(2)}) copy-start(f32[64,512]{1,0:T(8,128)} %get-tuple-element.66) | copy-start | bytes 393220
  89.2 8.5 %collective-permute-start.25 = (f32[64,1024]{1,0:T(8,128)S(1)}, f32[64,1024]{1,0:T(8,128)S(1)}, u32[]{:S(2)}, u32[]{:S(2)}) collective-permute-start(f32[64,1024]{1,0:T(8,128)S(1)} %slice_add_fusion), channel_id=1, source_target_pairs={{0,2},{1,3},{2,0},{3,1},{4,6},{5,7},{6,4},{7,5},{8,10},{9,11},{10,... | collective-permute-start | bytes 786440 | tf_op jit(solution)/shard_map/ppermute | solution.py:275
  97.7 7.6 %collective-permute-start.26 = (f32[64,1024]{1,0:T(8,128)S(1)}, f32[64,1024]{1,0:T(8,128)S(1)}, u32[]{:S(2)}, u32[]{:S(2)}) collective-permute-start(f32[64,1024]{1,0:T(8,128)S(1)} %fusion.5), channel_id=1, source_target_pairs={{0,4},{4,0},{8,12},{12,8},{16,20},{20,16},{24,28},{28,24},{1,5},{5... | collective-permute-start | bytes 786440 | tf_op jit(solution)/shard_map/ppermute | solution.py:275
  105.5 7.7 %collective-permute-start.27 = (f32[16,1024]{1,0:T(8,128)S(1)}, f32[16,1024]{1,0:T(8,128)S(1)}, u32[]{:S(2)}, u32[]{:S(2)}) collective-permute-start(f32[16,1024]{1,0:T(8,128)S(1)} %get-tuple-element.72), channel_id=1, source_target_pairs={{0,8},{4,12},{8,0},{12,4},{16,24},{20,28},{24,16},{28,20},{1,9},{5... | collective-permute-start | bytes 196616 | tf_op jit(solution)/shard_map/ppermute | solution.py:275
  105.5 7.6 %collective-permute-start.28 = (f32[16,1024]{1,0:T(8,128)S(1)}, f32[16,1024]{1,0:T(8,128)S(1)}, u32[]{:S(2)}, u32[]{:S(2)}) collective-permute-start(f32[16,1024]{1,0:T(8,128)S(1)} %get-tuple-element.70), channel_id=1, source_target_pairs={{0,16},{4,20},{8,24},{12,28},{16,0},{20,4},{24,8},{28,12},{1,17},{... | collective-permute-start | bytes 196616 | tf_op jit(solution)/shard_map/ppermute | solution.py:275
  108.0 6.3 %collective-permute-start.29 = (f32[16,1024]{1,0:T(8,128)S(1)}, f32[16,1024]{1,0:T(8,128)S(1)}, u32[]{:S(2)}, u32[]{:S(2)}) collective-permute-start(f32[16,1024]{1,0:T(8,128)S(1)} %get-tuple-element.71), channel_id=1, source_target_pairs={{0,24},{4,28},{8,16},{12,20},{16,8},{20,12},{24,0},{28,4},{1,25},{... | collective-permute-start | bytes 196616 | tf_op jit(solution)/shard_map/ppermute | solution.py:275
  114.3 11.3 %collective-permute-start.30 = (f32[16,1024]{1,0:T(8,128)S(1)}, f32[16,1024]{1,0:T(8,128)S(1)}, u32[]{:S(2)}, u32[]{:S(2)}) collective-permute-start(f32[16,1024]{1,0:T(8,128)S(1)} %add_add_fusion), channel_id=1, source_target_pairs={{0,8},{4,12},{8,0},{12,4},{16,24},{20,28},{24,16},{28,20},{1,9},{5... | collective-permute-start | bytes 196616 | tf_op jit(solution)/shard_map/ppermute | solution.py:275
  114.4 11.2 %collective-permute-start.31 = (f32[16,1024]{1,0:T(8,128)S(1)}, f32[16,1024]{1,0:T(8,128)S(1)}, u32[]{:S(2)}, u32[]{:S(2)}) collective-permute-start(f32[16,1024]{1,0:T(8,128)S(1)} %add_add_fusion), channel_id=1, source_target_pairs={{0,16},{4,20},{8,24},{12,28},{16,0},{20,4},{24,8},{28,12},{1,17},{... | collective-permute-start | bytes 196616 | tf_op jit(solution)/shard_map/ppermute | solution.py:275
  116.9 8.8 %collective-permute-start.32 = (f32[16,1024]{1,0:T(8,128)S(1)}, f32[16,1024]{1,0:T(8,128)S(1)}, u32[]{:S(2)}, u32[]{:S(2)}) collective-permute-start(f32[16,1024]{1,0:T(8,128)S(1)} %add_add_fusion), channel_id=1, source_target_pairs={{0,24},{4,28},{8,16},{12,20},{16,8},{20,12},{24,0},{28,4},{1,25},{... | collective-permute-start | bytes 196616 | tf_op jit(solution)/shard_map/ppermute | solution.py:275
